TPU v7x, 256 devices: a whole 4x4x8 slice. The times are simulated.
256 devices in a mesh: space: 8 (over y, core), chaos: 32 (over z, x).
Axes of the slice: x: 4, y: 4, z: 8, core: 2. Of those that a mesh axis runs over, the one named last changes fastest.
Arguments:
- source_term: float32 [480, 8, 64, 128], P('chaos', 'space'), may hold values from -17 to 17, as said below
- start_field: float32 [480, 8, 64, 128], P('chaos', 'space'), may hold values from -1.5 to 1.5
- conductivity: float32 [9, 8, 64, 128], P(None, 'space'), may hold values from -0.05 to 3, as said below
- pair_modes: int32 [8, 480, 2], replicated, may hold values from 0 to 479, as said below
- pair_weight: float32 [8, 480], replicated, may hold values from -1 to 1
Outputs:
- solution: float32 [480, 8, 64, 128], P('chaos', 'space')
- residual: float32 [480, 8, 64, 128], P('chaos', 'space')
- direction: float32 [480, 8, 64, 128], P('chaos', 'space')
Inputs may be any that keep to these rules, and one draw needn't show every extreme that they name: `source_term`: mode scales differ from mode to mode. conductivity[0] lies in 1 to 3 and every other coefficient field in -0.05 to 0.05. `pair_modes`: for each term, every mode appears in exactly two of the 480 pairs, and no pair joins a mode with itself.
All inputs are finite; a program needn't handle non-finite values.
Results may differ from a plain program's by a relative error of at most 0.0003.
Values sent between devices are 32-bit elements; how exact they have to be, the bound alone decides.
A program may use at most 320 MiB of HBM per device.

v0:
```python
import functools

import jax
import jax.numpy as jnp
from jax import lax
from jax.sharding import Mesh
from jax.sharding import PartitionSpec as P

SPACE = ("space_0", "space_1")
CHAOS = ("chaos_0", "chaos_1")
SPACE_CHAOS = ("space_0", "space_1", "chaos_0", "chaos_1")


CENTER_BOUND = 1.05
HALF_WIDTH = 0.95
FIRST_COEF = 4.0 * CENTER_BOUND / (2.0 * CENTER_BOUND * CENTER_BOUND - HALF_WIDTH * HALF_WIDTH)
SECOND_COEF = 2.0 / (2.0 * CENTER_BOUND * CENTER_BOUND - HALF_WIDTH * HALF_WIDTH)
NEIGHBOURS = ((1, 0, 0), (-1, 0, 0), (0, 1, 0), (0, -1, 0), (0, 0, 1), (0, 0, -1))
CENTER_OFFSET = (0, 0, 0)


def padded(x, sides, width):
    for axis, dim in sides:
        count, length = (lax.axis_size(axis), x.shape[dim])
        up = [(i, (i + 1) % count) for i in range(count - 1)]
        down = [(j, i) for i, j in up]
        last = lax.slice_in_dim(x, length - width, length, axis=dim)
        first = lax.slice_in_dim(x, 0, width, axis=dim)
        before = lax.ppermute(last, axis, up)
        after = lax.ppermute(first, axis, down)
        x = jnp.concatenate([before, x, after], axis=dim)
    return x


def one_axis_at_a_time(x, axes):
    return functools.reduce(lax.psum, axes, x)


def window(source, offset):
    extent = source.shape
    return source[
        ...,
        1 + offset[0] : extent[-3] - 1 + offset[0],
        1 + offset[1] : extent[-2] - 1 + offset[1],
        1 + offset[2] : extent[-1] - 1 + offset[2],
    ]


def stencil(coef_pad, field_pad):
    center_coef = window(coef_pad, CENTER_OFFSET)
    center_field = window(field_pad, CENTER_OFFSET)
    result = jnp.zeros_like(center_field)
    for offset in NEIGHBOURS:
        result = result + 0.5 * (center_coef + window(coef_pad, offset)) * (
            center_field - window(field_pad, offset)
        )
    return result


def diagonal_of(coef_pad):
    center_coef = window(coef_pad, CENTER_OFFSET)
    result = jnp.zeros_like(center_coef)
    for offset in NEIGHBOURS:
        result = result + 0.5 * (center_coef + window(coef_pad, offset))
    return result


def couple_modes(values, pair_list, weights):
    mode_count = values.shape[0]
    flattened = values.reshape(mode_count, -1)
    first_mode = pair_list[:, 0]
    second_mode = pair_list[:, 1]
    scaled = weights[:, None]
    mixed = jax.ops.segment_sum(
        scaled * flattened[second_mode], first_mode, num_segments=mode_count
    )
    mixed = mixed + jax.ops.segment_sum(
        scaled * flattened[first_mode], second_mode, num_segments=mode_count
    )
    return mixed.reshape(values.shape)


def pad_rows(values):
    return jnp.pad(values, ((0, 0), (0, 0), (1, 1), (1, 1)))


def per_device(source_term, start_field, conductivity, pair_modes, pair_weight):
    term_count = conductivity.shape[0]
    coef_rim = padded(conductivity, ((SPACE, 1),), 1)
    coef_pad = pad_rows(coef_rim)
    mean_pad = coef_pad[0]
    diagonal = diagonal_of(mean_pad)

    def precondition(values):
        scaled = values / diagonal
        scaled_pad = pad_rows(padded(scaled, ((SPACE, 1),), 1))
        return FIRST_COEF * scaled - SECOND_COEF * stencil(mean_pad, scaled_pad) / diagonal

    def operate(values):
        field_pad = pad_rows(padded(values, ((SPACE, 1),), 1))
        own_term = stencil(mean_pad, field_pad)
        stacked = jnp.stack(
            [stencil(coef_pad[term_index], field_pad) for term_index in range(1, term_count)]
        )
        received = lax.all_to_all(stacked, CHAOS, split_axis=3, concat_axis=1, tiled=True)
        summed = couple_modes(received[0], pair_modes[0], pair_weight[0])
        for term_index in range(1, term_count - 1):
            summed = summed + couple_modes(
                received[term_index], pair_modes[term_index], pair_weight[term_index]
            )
        coupled = lax.all_to_all(summed, CHAOS, split_axis=0, concat_axis=2, tiled=True)
        return own_term + coupled

    start_residual = source_term - operate(start_field)
    search = precondition(start_residual)
    image_field = operate(search)
    shaped_image = precondition(image_field)
    energy_start, curvature, image_energy = (
        one_axis_at_a_time(jnp.sum(start_residual * search), SPACE_CHAOS),
        one_axis_at_a_time(jnp.sum(search * image_field), SPACE_CHAOS),
        one_axis_at_a_time(jnp.sum(image_field * shaped_image), SPACE_CHAOS),
    )
    step_size = energy_start / curvature
    solution = start_field + step_size * search
    residual = start_residual - step_size * image_field
    new_search = search - step_size * shaped_image
    energy_next = energy_start - 2.0 * step_size * curvature + step_size * step_size * image_energy
    direction = new_search + energy_next / energy_start * search
    return (solution, residual, direction)


def solution(mesh):
    torus = Mesh(mesh.devices.reshape(4, 2, 8, 4), ("space_0", "space_1", "chaos_0", "chaos_1"))
    in_specs = (
        P(CHAOS, SPACE, None, None),
        P(CHAOS, SPACE, None, None),
        P(None, SPACE, None, None),
        P(),
        P(),
    )
    out_specs = (
        P(CHAOS, SPACE, None, None),
        P(CHAOS, SPACE, None, None),
        P(CHAOS, SPACE, None, None),
    )
    return jax.shard_map(
        per_device, mesh=torus, in_specs=in_specs, out_specs=out_specs, check_vma=False
    )
```

profile of v0, /device:TPU:32, one launch (start us, length us, event | category | flops | bytes accessed | tf_op | source)
XLA Modules:
  0.0 638.6 jit_solution(14969967797925912509)
XLA Ops:
  5.0 5.0 collective-permute-start.3
  21.1 4.2 copy.179
  25.3 11.8 %all-to-all-start = ((f32[8,15,1,64,128]{4,0,2,1,3:T(8,128)}), f32[8,15,1,64,128]{4,0,2,1,3:T(8,128)}, u32[]{:S(2)}, u32[]{:S(2)}) async-start(f32[8,15,1,64,128]{4,0,2,1,3:T(8,128)} %copy.179), calls=%async_computation | async-start | bytes 7864320 | tf_op jit(solution)/shard_map/all_to_all | solution.py:105
  39.9 84.7 %all-to-all-done = f32[8,15,1,64,128]{4,0,2,1,3:T(8,128)} async-done(((f32[8,15,1,64,128]{4,0,2,1,3:T(8,128)}), f32[8,15,1,64,128]{4,0,2,1,3:T(8,128)}, u32[]{:S(2)}, u32[]{:S(2)}) %all-to-all-start) | async-done | bytes 3932192 | tf_op jit(solution)/shard_map/all_to_all | solution.py:105
  124.7 4.1 copy.225
  136.0 7.4 %scatter_custom_fusion.15 = f32[480,256]{1,0:T(8,128)} fusion(s32[480]{0:T(512)} %bitcast.487, f32[480]{0:T(512)S(1)} %bitcast.437, f32[]{:T(128)} %constant.7.clone.1, f32[480,256]{1,0:T(8,128)} %bitcast.368, s32[1024]{0:T(1024)S(1)} %pad_clamp_fusion), kind=kCustom, calls=%fused_computation.202 | custom fusion | flops 245760 | bytes 989568 | tf_op jit(solution)/shard_map/scatter-add | solution.py:77
  143.4 7.2 %scatter_custom_fusion.14 = f32[480,256]{1,0:T(8,128)} fusion(s32[480]{0:T(512)} %bitcast.485, f32[480]{0:T(512)S(1)} %bitcast.438, f32[]{:T(128)} %constant.7.clone.1, f32[480,256]{1,0:T(8,128)} %bitcast.369, s32[1024]{0:T(1024)S(1)} %pad_clamp_fusion.1), kind=kCustom, calls=%fused_computation.204 | custom fusion | flops 245760 | bytes 989568 | tf_op jit(solution)/shard_map/scatter-add | solution.py:74
  150.6 7.5 %scatter_custom_fusion.1 = f32[480,256]{1,0:T(8,128)} fusion(s32[480]{0:T(512)} %bitcast.479, f32[480]{0:T(512)S(1)} %bitcast.433, f32[]{:T(128)} %constant.7.clone.1, f32[480,256]{1,0:T(8,128)} %bitcast.364, s32[1024]{0:T(1024)S(1)} %pad_clamp_fusion.14), kind=kCustom, calls=%fused_computation.230 | custom fusion | flops 245760 | bytes 989568 | tf_op jit(solution)/shard_map/scatter-add | solution.py:77
  158.1 7.1 %scatter_custom_fusion = f32[480,256]{1,0:T(8,128)} fusion(s32[480]{0:T(512)} %bitcast.473, f32[480]{0:T(512)S(1)} %bitcast.434, f32[]{:T(128)} %constant.7.clone.1, f32[480,256]{1,0:T(8,128)} %bitcast.365, s32[1024]{0:T(1024)S(1)} %pad_clamp_fusion.15), kind=kCustom, calls=%fused_computation.232 | custom fusion | flops 245760 | bytes 989568 | tf_op jit(solution)/shard_map/scatter-add | solution.py:74
  165.2 7.2 %scatter_custom_fusion.13 = f32[480,256]{1,0:T(8,128)} fusion(s32[480]{0:T(512)} %bitcast.483, f32[480]{0:T(512)S(1)} %bitcast.429, f32[]{:T(128)} %constant.7.clone.1, f32[480,256]{1,0:T(8,128)} %bitcast.366, s32[1024]{0:T(1024)S(1)} %pad_clamp_fusion.2), kind=kCustom, calls=%fused_computation.206 | custom fusion | flops 245760 | bytes 989568 | tf_op jit(solution)/shard_map/scatter-add | solution.py:77
  172.4 7.0 %scatter_custom_fusion.12 = f32[480,256]{1,0:T(8,128)} fusion(s32[480]{0:T(512)} %bitcast.481, f32[480]{0:T(512)S(1)} %bitcast.430, f32[]{:T(128)} %constant.7.clone.1, f32[480,256]{1,0:T(8,128)} %bitcast.367, s32[1024]{0:T(1024)S(1)} %pad_clamp_fusion.3), kind=kCustom, calls=%fused_computation.208 | custom fusion | flops 245760 | bytes 989568 | tf_op jit(solution)/shard_map/scatter-add | solution.py:74
  179.5 7.3 %scatter_custom_fusion.11 = f32[480,256]{1,0:T(8,128)} fusion(s32[480]{0:T(512)} %bitcast.477, f32[480]{0:T(512)S(1)} %bitcast.425, f32[]{:T(128)} %constant.7.clone.1, f32[480,256]{1,0:T(8,128)} %bitcast.362, s32[1024]{0:T(1024)S(1)} %pad_clamp_fusion.4), kind=kCustom, calls=%fused_computation.210 | custom fusion | flops 245760 | bytes 989568 | tf_op jit(solution)/shard_map/scatter-add | solution.py:77
  186.8 7.1 %scatter_custom_fusion.10 = f32[480,256]{1,0:T(8,128)} fusion(s32[480]{0:T(512)} %bitcast.471, f32[480]{0:T(512)S(1)} %bitcast.426, f32[]{:T(128)} %constant.7.clone.1, f32[480,256]{1,0:T(8,128)} %bitcast.363, s32[1024]{0:T(1024)S(1)} %pad_clamp_fusion.5), kind=kCustom, calls=%fused_computation.212 | custom fusion | flops 245760 | bytes 989568 | tf_op jit(solution)/shard_map/scatter-add | solution.py:74
  193.8 7.3 %scatter_custom_fusion.9 = f32[480,256]{1,0:T(8,128)} fusion(s32[480]{0:T(512)} %bitcast.467, f32[480]{0:T(512)S(1)} %bitcast.421, f32[]{:T(128)} %constant.7.clone.1, f32[480,256]{1,0:T(8,128)} %bitcast.360, s32[1024]{0:T(1024)S(1)} %pad_clamp_fusion.6), kind=kCustom, calls=%fused_computation.214 | custom fusion | flops 245760 | bytes 989568 | tf_op jit(solution)/shard_map/scatter-add | solution.py:77
  201.1 7.0 %scatter_custom_fusion.8 = f32[480,256]{1,0:T(8,128)} fusion(s32[480]{0:T(512)} %bitcast.463, f32[480]{0:T(512)S(1)} %bitcast.422, f32[]{:T(128)} %constant.7.clone.1, f32[480,256]{1,0:T(8,128)} %bitcast.361, s32[1024]{0:T(1024)S(1)} %pad_clamp_fusion.7), kind=kCustom, calls=%fused_computation.216 | custom fusion | flops 245760 | bytes 989568 | tf_op jit(solution)/shard_map/scatter-add | solution.py:74
  208.2 7.5 %scatter_custom_fusion.7 = f32[480,256]{1,0:T(8,128)} fusion(s32[480]{0:T(512)} %bitcast.475, f32[480]{0:T(512)S(1)} %bitcast.417, f32[]{:T(128)} %constant.7.clone.1, f32[480,256]{1,0:T(8,128)} %bitcast.358, s32[1024]{0:T(1024)S(1)} %pad_clamp_fusion.8), kind=kCustom, calls=%fused_computation.218 | custom fusion | flops 245760 | bytes 989568 | tf_op jit(solution)/shard_map/scatter-add | solution.py:77
  215.7 7.0 %scatter_custom_fusion.6 = f32[480,256]{1,0:T(8,128)} fusion(s32[480]{0:T(512)} %bitcast.469, f32[480]{0:T(512)S(1)} %bitcast.418, f32[]{:T(128)} %constant.7.clone.1, f32[480,256]{1,0:T(8,128)} %bitcast.359, s32[1024]{0:T(1024)S(1)} %pad_clamp_fusion.9), kind=kCustom, calls=%fused_computation.220 | custom fusion | flops 245760 | bytes 989568 | tf_op jit(solution)/shard_map/scatter-add | solution.py:74
  222.8 7.2 %scatter_custom_fusion.5 = f32[480,256]{1,0:T(8,128)} fusion(s32[480]{0:T(512)} %bitcast.465, f32[480]{0:T(512)S(1)} %bitcast.413, f32[]{:T(128)} %constant.7.clone.1, f32[480,256]{1,0:T(8,128)} %bitcast.356, s32[1024]{0:T(1024)S(1)} %pad_clamp_fusion.10), kind=kCustom, calls=%fused_computation.222 | custom fusion | flops 245760 | bytes 989568 | tf_op jit(solution)/shard_map/scatter-add | solution.py:77
  230.0 7.1 %scatter_custom_fusion.4 = f32[480,256]{1,0:T(8,128)} fusion(s32[480]{0:T(512)} %bitcast.461, f32[480]{0:T(512)S(1)} %bitcast.414, f32[]{:T(128)} %constant.7.clone.1, f32[480,256]{1,0:T(8,128)} %bitcast.357, s32[1024]{0:T(1024)S(1)} %pad_clamp_fusion.11), kind=kCustom, calls=%fused_computation.224 | custom fusion | flops 245760 | bytes 989568 | tf_op jit(solution)/shard_map/scatter-add | solution.py:74
  237.1 4.9 scatter_custom_fusion.3
  242.0 5.1 scatter_custom_fusion.2
  251.9 9.1 %all-to-all-start.1 = ((f32[480,1,2,128]{3,2,1,0:T(2,128)}), f32[480,1,2,128]{3,2,1,0:T(2,128)S(1)}, u32[]{:S(2)}, u32[]{:S(2)}) async-start(f32[480,1,2,128]{3,2,1,0:T(2,128)} %reshape.441), calls=%async_computation.1 | async-start | bytes 983040 | tf_op jit(solution)/shard_map/all_to_all | solution.py:111
  262.9 14.9 %all-to-all-done.1 = f32[480,1,2,128]{3,2,1,0:T(2,128)S(1)} async-done(((f32[480,1,2,128]{3,2,1,0:T(2,128)}), f32[480,1,2,128]{3,2,1,0:T(2,128)S(1)}, u32[]{:S(2)}, u32[]{:S(2)}) %all-to-all-start.1) | async-done | bytes 491552 | tf_op jit(solution)/shard_map/all_to_all | solution.py:111
  287.2 8.8 %collective-permute-start.7 = (f32[15,1,64,128]{3,2,0,1:T(8,128)S(1)}, f32[15,1,64,128]{3,2,0,1:T(8,128)S(1)}, u32[]{:S(2)}, u32[]{:S(2)}) collective-permute-start(f32[15,1,64,128]{3,2,0,1:T(8,128)S(1)} %fusion.21), channel_id=1, source_target_pairs={{0,32},{32,64},{64,96},{96,128},{128,160},{160,192},{192,224},{1,3... | collective-permute-start | bytes 1474568 | tf_op jit(solution)/shard_map/ppermute | solution.py:29
  297.5 4.3 collective-permute-done.6
  310.5 89.6 %all_to_all.66 = f32[8,15,1,64,128]{4,0,2,1,3:T(8,128)S(1)} all-to-all(f32[8,15,1,64,128]{4,0,2,1,3:T(8,128)S(1)} %copy.183), channel_id=1, replica_groups=mesh['space_0'=4,'space_1'=2,'chaos_0'=8,'chaos_1'=4] {'chaos_0','chaos_1'}, dimensions={3} | all-to-all | bytes 7864320 | tf_op jit(solution)/shard_map/all_to_all | solution.py:105
  405.2 7.4 %scatter_custom_fusion.31 = f32[480,256]{1,0:T(8,128)} fusion(s32[480]{0:T(512)} %bitcast.488, f32[480]{0:T(512)} %bitcast.439, f32[]{:T(128)} %constant.7.clone.1, f32[480,256]{1,0:T(8,128)} %bitcast.372, s32[1024]{0:T(1024)} %copy-done.111), kind=kCustom, calls=%fused_computation.168 | custom fusion | flops 245760 | bytes 989696 | tf_op jit(solution)/shard_map/scatter-add | solution.py:77
  412.6 7.2 %scatter_custom_fusion.30 = f32[480,256]{1,0:T(8,128)} fusion(s32[480]{0:T(512)} %bitcast.486, f32[480]{0:T(512)} %bitcast.440, f32[]{:T(128)} %constant.7.clone.1, f32[480,256]{1,0:T(8,128)} %bitcast.373, s32[1024]{0:T(1024)} %copy-done.110), kind=kCustom, calls=%fused_computation.170 | custom fusion | flops 245760 | bytes 989696 | tf_op jit(solution)/shard_map/scatter-add | solution.py:74
  421.7 7.4 %scatter_custom_fusion.17 = f32[480,256]{1,0:T(8,128)} fusion(s32[480]{0:T(512)} %bitcast.480, f32[480]{0:T(512)} %bitcast.435, f32[]{:T(128)} %constant.7.clone.1, f32[480,256]{1,0:T(8,128)} %bitcast.374, s32[1024]{0:T(1024)} %copy-done.107), kind=kCustom, calls=%fused_computation.196 | custom fusion | flops 245760 | bytes 989696 | tf_op jit(solution)/shard_map/scatter-add | solution.py:77
  429.1 7.2 %scatter_custom_fusion.16 = f32[480,256]{1,0:T(8,128)} fusion(s32[480]{0:T(512)} %bitcast.474, f32[480]{0:T(512)} %bitcast.436, f32[]{:T(128)} %constant.7.clone.1, f32[480,256]{1,0:T(8,128)} %bitcast.375, s32[1024]{0:T(1024)} %copy-done.105), kind=kCustom, calls=%fused_computation.198 | custom fusion | flops 245760 | bytes 989696 | tf_op jit(solution)/shard_map/scatter-add | solution.py:74
  438.1 7.6 %scatter_custom_fusion.29 = f32[480,256]{1,0:T(8,128)} fusion(s32[480]{0:T(512)} %bitcast.484, f32[480]{0:T(512)} %bitcast.431, f32[]{:T(128)} %constant.7.clone.1, f32[480,256]{1,0:T(8,128)} %bitcast.376, s32[1024]{0:T(1024)} %copy-done.109), kind=kCustom, calls=%fused_computation.172 | custom fusion | flops 245760 | bytes 989696 | tf_op jit(solution)/shard_map/scatter-add | solution.py:77
  445.7 7.3 %scatter_custom_fusion.28 = f32[480,256]{1,0:T(8,128)} fusion(s32[480]{0:T(512)} %bitcast.482, f32[480]{0:T(512)} %bitcast.432, f32[]{:T(128)} %constant.7.clone.1, f32[480,256]{1,0:T(8,128)} %bitcast.377, s32[1024]{0:T(1024)} %copy-done.108), kind=kCustom, calls=%fused_computation.174 | custom fusion | flops 245760 | bytes 989696 | tf_op jit(solution)/shard_map/scatter-add | solution.py:74
  454.9 7.8 %scatter_custom_fusion.27 = f32[480,256]{1,0:T(8,128)} fusion(s32[480]{0:T(512)} %bitcast.478, f32[480]{0:T(512)} %bitcast.427, f32[]{:T(128)} %constant.7.clone.1, f32[480,256]{1,0:T(8,128)} %bitcast.378, s32[1024]{0:T(1024)} %copy-done.106), kind=kCustom, calls=%fused_computation.176 | custom fusion | flops 245760 | bytes 989696 | tf_op jit(solution)/shard_map/scatter-add | solution.py:77
  462.7 7.3 %scatter_custom_fusion.26 = f32[480,256]{1,0:T(8,128)} fusion(s32[480]{0:T(512)} %bitcast.472, f32[480]{0:T(512)} %bitcast.428, f32[]{:T(128)} %constant.7.clone.1, f32[480,256]{1,0:T(8,128)} %bitcast.379, s32[1024]{0:T(1024)} %copy-done.103), kind=kCustom, calls=%fused_computation.178 | custom fusion | flops 245760 | bytes 989696 | tf_op jit(solution)/shard_map/scatter-add | solution.py:74
  471.9 7.4 %scatter_custom_fusion.25 = f32[480,256]{1,0:T(8,128)} fusion(s32[480]{0:T(512)} %bitcast.468, f32[480]{0:T(512)S(1)} %bitcast.423, f32[]{:T(128)} %constant.7.clone.1, f32[480,256]{1,0:T(8,128)} %bitcast.380, s32[1024]{0:T(1024)} %copy-done.101), kind=kCustom, calls=%fused_computation.180 | custom fusion | flops 245760 | bytes 989568 | tf_op jit(solution)/shard_map/scatter-add | solution.py:77
  479.2 7.2 %scatter_custom_fusion.24 = f32[480,256]{1,0:T(8,128)} fusion(s32[480]{0:T(512)} %bitcast.464, f32[480]{0:T(512)S(1)} %bitcast.424, f32[]{:T(128)} %constant.7.clone.1, f32[480,256]{1,0:T(8,128)} %bitcast.381, s32[1024]{0:T(1024)} %copy-done.99), kind=kCustom, calls=%fused_computation.182 | custom fusion | flops 245760 | bytes 989568 | tf_op jit(solution)/shard_map/scatter-add | solution.py:74
  488.3 7.4 %scatter_custom_fusion.23 = f32[480,256]{1,0:T(8,128)} fusion(s32[480]{0:T(512)} %bitcast.476, f32[480]{0:T(512)S(1)} %bitcast.419, f32[]{:T(128)} %constant.7.clone.1, f32[480,256]{1,0:T(8,128)} %bitcast.382, s32[1024]{0:T(1024)} %copy-done.104), kind=kCustom, calls=%fused_computation.184 | custom fusion | flops 245760 | bytes 989568 | tf_op jit(solution)/shard_map/scatter-add | solution.py:77
  495.7 7.2 %scatter_custom_fusion.22 = f32[480,256]{1,0:T(8,128)} fusion(s32[480]{0:T(512)} %bitcast.470, f32[480]{0:T(512)S(1)} %bitcast.420, f32[]{:T(128)} %constant.7.clone.1, f32[480,256]{1,0:T(8,128)} %bitcast.383, s32[1024]{0:T(1024)} %copy-done.102), kind=kCustom, calls=%fused_computation.186 | custom fusion | flops 245760 | bytes 989568 | tf_op jit(solution)/shard_map/scatter-add | solution.py:74
  504.8 7.4 %scatter_custom_fusion.21 = f32[480,256]{1,0:T(8,128)} fusion(s32[480]{0:T(512)} %bitcast.466, f32[480]{0:T(512)S(1)} %bitcast.415, f32[]{:T(128)} %constant.7.clone.1, f32[480,256]{1,0:T(8,128)} %bitcast.384, s32[1024]{0:T(1024)} %copy-done.100), kind=kCustom, calls=%fused_computation.188 | custom fusion | flops 245760 | bytes 989568 | tf_op jit(solution)/shard_map/scatter-add | solution.py:77
  512.2 7.2 %scatter_custom_fusion.20 = f32[480,256]{1,0:T(8,128)} fusion(s32[480]{0:T(512)} %bitcast.462, f32[480]{0:T(512)S(1)} %bitcast.416, f32[]{:T(128)} %constant.7.clone.1, f32[480,256]{1,0:T(8,128)} %bitcast.385, s32[1024]{0:T(1024)} %copy-done.98), kind=kCustom, calls=%fused_computation.190 | custom fusion | flops 245760 | bytes 989568 | tf_op jit(solution)/shard_map/scatter-add | solution.py:74
  521.2 7.5 %scatter_custom_fusion.19 = f32[480,256]{1,0:T(8,128)} fusion(s32[480]{0:T(512)} %bitcast.460, f32[480]{0:T(512)S(1)} %bitcast.411, f32[]{:T(128)} %constant.7.clone.1, f32[480,256]{1,0:T(8,128)} %bitcast.370, s32[1024]{0:T(1024)} %copy-done.97), kind=kCustom, calls=%fused_computation.192 | custom fusion | flops 245760 | bytes 989568 | tf_op jit(solution)/shard_map/scatter-add | solution.py:77
  528.7 7.2 %scatter_custom_fusion.18 = f32[480,256]{1,0:T(8,128)} fusion(s32[480]{0:T(512)} %bitcast.458, f32[480]{0:T(512)S(1)} %bitcast.412, f32[]{:T(128)} %constant.7.clone.1, f32[480,256]{1,0:T(8,128)} %bitcast.371, s32[1024]{0:T(1024)S(1)} %copy-done.96), kind=kCustom, calls=%fused_computation.194 | custom fusion | flops 245760 | bytes 989568 | tf_op jit(solution)/shard_map/scatter-add | solution.py:74
  535.9 4.5 add_add_fusion
  542.5 22.5 %all_to_all.67 = f32[480,1,2,128]{3,2,1,0:T(2,128)S(1)} all-to-all(f32[480,1,2,128]{3,2,1,0:T(2,128)} %reshape.442), channel_id=1, replica_groups=mesh['space_0'=4,'space_1'=2,'chaos_0'=8,'chaos_1'=4] {'chaos_0','chaos_1'}, dimensions={0} | all-to-all | bytes 983040 | tf_op jit(solution)/shard_map/all_to_all | solution.py:111
  567.9 6.1 collective-permute-start.9
  577.9 24.3 %all-reduce.7 = (f32[]{:T(128)}, f32[]{:T(128)}, f32[]{:T(128)}) all-reduce(f32[]{:T(128)} %get-tuple-element.20, f32[]{:T(128)} %get-tuple-element.19, f32[]{:T(128)} %get-tuple-element.18), channel_id=1, replica_groups=mesh['space_0'=4,'space_1'=2,'chaos_0'=8,'chaos_1'=4] {'space_0'}, use_global_device_ids=true, to_apply=%region_17.18 | all-reduce | flops 3 | bytes 24 | tf_op jit(solution)/shard_map/psum | solution.py:36
  605.3 15.5 %all-reduce.5 = (f32[]{:T(128)}, f32[]{:T(128)}, f32[]{:T(128)}) all-reduce(f32[]{:T(128)} %get-tuple-element.30, f32[]{:T(128)} %get-tuple-element.31, f32[]{:T(128)} %get-tuple-element.32), channel_id=1, replica_groups=mesh['space_0'=4,'space_1'=2,'chaos_0'=8,'chaos_1'=4] {'chaos_0'}, use_global_device_ids=true, to_apply=%region_19.20 | all-reduce | flops 3 | bytes 24 | tf_op jit(solution)/shard_map/psum | solution.py:36
  620.9 10.4 %all-reduce.6 = (f32[]{:T(128)}, f32[]{:T(128)}, f32[]{:T(128)}) all-reduce(f32[]{:T(128)} %get-tuple-element.21, f32[]{:T(128)} %get-tuple-element.22, f32[]{:T(128)} %get-tuple-element.23), channel_id=1, replica_groups=mesh['space_0'=4,'space_1'=2,'chaos_0'=8,'chaos_1'=4] {'chaos_1'}, use_global_device_ids=true, to_apply=%region_20.21 | all-reduce | flops 3 | bytes 24 | tf_op jit(solution)/shard_map/psum | solution.py:36
  (329 shorter events, 82.8 us)
Async XLA Ops:
  0.6 9.4 %collective-permute-start = (f32[9,1,64,128]{3,2,1,0:T(8,128)}, f32[9,1,64,128]{3,2,1,0:T(8,128)S(1)}, u32[]{:S(2)}, u32[]{:S(2)}) collective-permute-start(f32[9,1,64,128]{3,2,1,0:T(8,128)} %param.7), channel_id=1, source_target_pairs={{0,32},{32,64},{64,96},{96,128},{128,160},{160,192},{192,224},{1,3... | collective-permute-start | bytes 884744 | tf_op jit(solution)/shard_map/ppermute | solution.py:29
  2.4 7.7 %collective-permute-start.1 = (f32[9,1,64,128]{3,2,1,0:T(8,128)}, f32[9,1,64,128]{3,2,1,0:T(8,128)S(1)}, u32[]{:S(2)}, u32[]{:S(2)}) collective-permute-start(f32[9,1,64,128]{3,2,1,0:T(8,128)} %param.7), channel_id=1, source_target_pairs={{32,0},{64,32},{96,64},{128,96},{160,128},{192,160},{224,192},{33,... | collective-permute-start | bytes 884744 | tf_op jit(solution)/shard_map/ppermute | solution.py:30
  3.7 11.4 %collective-permute-start.2 = (f32[15,1,64,128]{3,2,0,1:T(8,128)}, f32[15,1,64,128]{3,2,0,1:T(8,128)S(1)}, u32[]{:S(2)}, u32[]{:S(2)}) collective-permute-start(f32[15,1,64,128]{3,2,0,1:T(8,128)} %bitcast.386), channel_id=1, source_target_pairs={{32,0},{64,32},{96,64},{128,96},{160,128},{192,160},{224,192},{33,... | collective-permute-start | bytes 1474568 | tf_op jit(solution)/shard_map/ppermute | solution.py:30
  5.0 10.1 %collective-permute-start.3 = (f32[15,1,64,128]{3,2,0,1:T(8,128)}, f32[15,1,64,128]{3,2,0,1:T(8,128)S(1)}, u32[]{:S(2)}, u32[]{:S(2)}) collective-permute-start(f32[15,1,64,128]{3,2,0,1:T(8,128)} %bitcast.387), channel_id=1, source_target_pairs={{0,32},{32,64},{64,96},{96,128},{128,160},{160,192},{192,224},{1,3... | collective-permute-start | bytes 1474568 | tf_op jit(solution)/shard_map/ppermute | solution.py:29
  12.6 8.1 %copy-start.13 = (f32[64,128]{1,0:T(8,128)}, f32[64,128]{1,0:T(8,128)S(1)}, u32[]{:S(2)}) copy-start(f32[64,128]{1,0:T(8,128)S(1)} %get-tuple-element.86) | copy-start | bytes 98308
  12.6 8.1 %copy-start.15 = (f32[64,128]{1,0:T(8,128)}, f32[64,128]{1,0:T(8,128)S(1)}, u32[]{:S(2)}) copy-start(f32[64,128]{1,0:T(8,128)S(1)} %get-tuple-element.87) | copy-start | bytes 98308
  12.6 8.1 %copy-start.17 = (f32[64,128]{1,0:T(8,128)}, f32[64,128]{1,0:T(8,128)S(1)}, u32[]{:S(2)}) copy-start(f32[64,128]{1,0:T(8,128)S(1)} %get-tuple-element.88) | copy-start | bytes 98308
  12.6 8.1 %copy-start.19 = (f32[64,128]{1,0:T(8,128)}, f32[64,128]{1,0:T(8,128)S(1)}, u32[]{:S(2)}) copy-start(f32[64,128]{1,0:T(8,128)S(1)} %get-tuple-element.89) | copy-start | bytes 98308
  12.6 8.1 %copy-start.21 = (f32[64,128]{1,0:T(8,128)}, f32[64,128]{1,0:T(8,128)S(1)}, u32[]{:S(2)}) copy-start(f32[64,128]{1,0:T(8,128)S(1)} %get-tuple-element.90) | copy-start | bytes 98308
  12.6 8.1 %copy-start.23 = (f32[64,128]{1,0:T(8,128)}, f32[64,128]{1,0:T(8,128)S(1)}, u32[]{:S(2)}) copy-start(f32[64,128]{1,0:T(8,128)S(1)} %get-tuple-element.91) | copy-start | bytes 98308
  25.3 11.8 %copy-start.112 = (s32[8,480,2]{1,2,0:T(2,128)S(1)}, s32[8,480,2]{1,2,0:T(2,128)}, u32[]{:S(2)}) copy-start(s32[8,480,2]{1,2,0:T(2,128)} %param.8) | copy-start | bytes 92164
  25.3 14.5 %copy-start.113 = (f32[8,480]{1,0:T(8,128)S(1)}, f32[8,480]{1,0:T(8,128)}, u32[]{:S(2)}) copy-start(f32[8,480]{1,0:T(8,128)} %param.9) | copy-start | bytes 46084
  25.3 99.3 %all-to-all-start = ((f32[8,15,1,64,128]{4,0,2,1,3:T(8,128)}), f32[8,15,1,64,128]{4,0,2,1,3:T(8,128)}, u32[]{:S(2)}, u32[]{:S(2)}) async-start(f32[8,15,1,64,128]{4,0,2,1,3:T(8,128)} %copy.179), calls=%async_computation | async-start | bytes 7864320 | tf_op jit(solution)/shard_map/all_to_all | solution.py:105
  37.7 204.3 %copy-start.95 = (s32[1024]{0:T(1024)}, s32[1024]{0:T(1024)S(1)}, u32[]{:S(2)}) copy-start(s32[1024]{0:T(1024)S(1)} %pad_clamp_fusion.13) | copy-start | bytes 12292
  37.8 199.3 %copy-start.97 = (s32[1024]{0:T(1024)}, s32[1024]{0:T(1024)S(1)}, u32[]{:S(2)}) copy-start(s32[1024]{0:T(1024)S(1)} %pad_clamp_fusion.12) | copy-start | bytes 12292
  37.8 120.3 %copy-start.105 = (s32[1024]{0:T(1024)}, s32[1024]{0:T(1024)S(1)}, u32[]{:S(2)}) copy-start(s32[1024]{0:T(1024)S(1)} %pad_clamp_fusion.15) | copy-start | bytes 12292
  37.8 112.8 %copy-start.107 = (s32[1024]{0:T(1024)}, s32[1024]{0:T(1024)S(1)}, u32[]{:S(2)}) copy-start(s32[1024]{0:T(1024)S(1)} %pad_clamp_fusion.14) | copy-start | bytes 12292
  38.4 148.3 %copy-start.103 = (s32[1024]{0:T(1024)}, s32[1024]{0:T(1024)S(1)}, u32[]{:S(2)}) copy-start(s32[1024]{0:T(1024)S(1)} %pad_clamp_fusion.5) | copy-start | bytes 12292
  38.4 141.1 %copy-start.106 = (s32[1024]{0:T(1024)}, s32[1024]{0:T(1024)S(1)}, u32[]{:S(2)}) copy-start(s32[1024]{0:T(1024)S(1)} %pad_clamp_fusion.4) | copy-start | bytes 12292
  38.4 162.7 %copy-start.99 = (s32[1024]{0:T(1024)}, s32[1024]{0:T(1024)S(1)}, u32[]{:S(2)}) copy-start(s32[1024]{0:T(1024)S(1)} %pad_clamp_fusion.7) | copy-start | bytes 12292
  38.5 155.4 %copy-start.101 = (s32[1024]{0:T(1024)}, s32[1024]{0:T(1024)S(1)}, u32[]{:S(2)}) copy-start(s32[1024]{0:T(1024)S(1)} %pad_clamp_fusion.6) | copy-start | bytes 12292
  39.1 176.6 %copy-start.102 = (s32[1024]{0:T(1024)}, s32[1024]{0:T(1024)S(1)}, u32[]{:S(2)}) copy-start(s32[1024]{0:T(1024)S(1)} %pad_clamp_fusion.9) | copy-start | bytes 12292
  39.1 169.1 %copy-start.104 = (s32[1024]{0:T(1024)}, s32[1024]{0:T(1024)S(1)}, u32[]{:S(2)}) copy-start(s32[1024]{0:T(1024)S(1)} %pad_clamp_fusion.8) | copy-start | bytes 12292
  39.1 190.9 %copy-start.98 = (s32[1024]{0:T(1024)}, s32[1024]{0:T(1024)S(1)}, u32[]{:S(2)}) copy-start(s32[1024]{0:T(1024)S(1)} %pad_clamp_fusion.11) | copy-start | bytes 12292
  39.2 183.6 %copy-start.100 = (s32[1024]{0:T(1024)}, s32[1024]{0:T(1024)S(1)}, u32[]{:S(2)}) copy-start(s32[1024]{0:T(1024)S(1)} %pad_clamp_fusion.10) | copy-start | bytes 12292
  39.8 103.6 %copy-start.110 = (s32[1024]{0:T(1024)}, s32[1024]{0:T(1024)S(1)}, u32[]{:S(2)}) copy-start(s32[1024]{0:T(1024)S(1)} %pad_clamp_fusion.1) | copy-start | bytes 12292
  39.8 96.2 %copy-start.111 = (s32[1024]{0:T(1024)}, s32[1024]{0:T(1024)S(1)}, u32[]{:S(2)}) copy-start(s32[1024]{0:T(1024)S(1)} %pad_clamp_fusion) | copy-start | bytes 12292
  39.8 132.6 %copy-start.108 = (s32[1024]{0:T(1024)}, s32[1024]{0:T(1024)S(1)}, u32[]{:S(2)}) copy-start(s32[1024]{0:T(1024)S(1)} %pad_clamp_fusion.3) | copy-start | bytes 12292
  39.9 125.3 %copy-start.109 = (s32[1024]{0:T(1024)}, s32[1024]{0:T(1024)S(1)}, u32[]{:S(2)}) copy-start(s32[1024]{0:T(1024)S(1)} %pad_clamp_fusion.2) | copy-start | bytes 12292
  39.9 103.5 %copy-start.94 = (f32[1,480]{1,0:T(1,128)}, f32[1,480]{1,0:T(1,128)S(1)}, u32[]{:S(2)}) copy-start(f32[1,480]{1,0:T(1,128)S(1)} %get-tuple-element.148) | copy-start | bytes 5764
  39.9 118.2 %copy-start.93 = (f32[1,480]{1,0:T(1,128)}, f32[1,480]{1,0:T(1,128)S(1)}, u32[]{:S(2)}) copy-start(f32[1,480]{1,0:T(1,128)S(1)} %get-tuple-element.142) | copy-start | bytes 5764
  39.9 132.5 %copy-start.92 = (f32[1,480]{1,0:T(1,128)}, f32[1,480]{1,0:T(1,128)S(1)}, u32[]{:S(2)}) copy-start(f32[1,480]{1,0:T(1,128)S(1)} %get-tuple-element.149) | copy-start | bytes 5764
  39.9 146.8 %copy-start.91 = (f32[1,480]{1,0:T(1,128)}, f32[1,480]{1,0:T(1,128)S(1)}, u32[]{:S(2)}) copy-start(f32[1,480]{1,0:T(1,128)S(1)} %get-tuple-element.143) | copy-start | bytes 5764
  251.9 25.9 %all-to-all-start.1 = ((f32[480,1,2,128]{3,2,1,0:T(2,128)}), f32[480,1,2,128]{3,2,1,0:T(2,128)S(1)}, u32[]{:S(2)}, u32[]{:S(2)}) async-start(f32[480,1,2,128]{3,2,1,0:T(2,128)} %reshape.441), calls=%async_computation.1 | async-start | bytes 983040 | tf_op jit(solution)/shard_map/all_to_all | solution.py:111
  279.7 4.5 collective-permute-start.4
  281.1 4.5 collective-permute-start.5
  287.2 10.2 %collective-permute-start.7 = (f32[15,1,64,128]{3,2,0,1:T(8,128)S(1)}, f32[15,1,64,128]{3,2,0,1:T(8,128)S(1)}, u32[]{:S(2)}, u32[]{:S(2)}) collective-permute-start(f32[15,1,64,128]{3,2,0,1:T(8,128)S(1)} %fusion.21), channel_id=1, source_target_pairs={{0,32},{32,64},{64,96},{96,128},{128,160},{160,192},{192,224},{1,3... | collective-permute-start | bytes 1474568 | tf_op jit(solution)/shard_map/ppermute | solution.py:29
  296.0 5.7 collective-permute-start.6
  488.3 40.4 %copy-start.96 = (s32[1024]{0:T(1024)S(1)}, s32[1024]{0:T(1024)}, u32[]{:S(2)}) copy-start(s32[1024]{0:T(1024)} %copy-done.95) | copy-start | bytes 12292
  566.4 11.5 %copy-start.4 = (f32[15,1,64,128]{3,2,0,1:T(8,128)}, f32[15,1,64,128]{3,2,0,1:T(8,128)S(1)}, u32[]{:S(2)}) copy-start(f32[15,1,64,128]{3,2,0,1:T(8,128)S(1)} %get-tuple-element.35) | copy-start | bytes 1474564
  566.4 10.0 %copy-start.1 = (f32[15,1,64,128]{3,2,0,1:T(8,128)S(1)}, f32[15,1,64,128]{3,2,0,1:T(8,128)}, u32[]{:S(2)}) copy-start(f32[15,1,64,128]{3,2,0,1:T(8,128)} %copy-done) | copy-start | bytes 1474564
  566.4 10.0 %copy-start.6 = (f32[64,128]{1,0:T(8,128)S(1)}, f32[64,128]{1,0:T(8,128)}, u32[]{:S(2)}) copy-start(f32[64,128]{1,0:T(8,128)} %get-tuple-element.82) | copy-start | bytes 98308
  566.4 10.0 %copy-start.8 = (f32[64,128]{1,0:T(8,128)S(1)}, f32[64,128]{1,0:T(8,128)}, u32[]{:S(2)}) copy-start(f32[64,128]{1,0:T(8,128)} %get-tuple-element.83) | copy-start | bytes 98308
  566.5 10.0 %copy-start.10 = (f32[64,128]{1,0:T(8,128)S(1)}, f32[64,128]{1,0:T(8,128)}, u32[]{:S(2)}) copy-start(f32[64,128]{1,0:T(8,128)} %get-tuple-element.84) | copy-start | bytes 98308
  566.5 10.0 %copy-start.12 = (f32[64,128]{1,0:T(8,128)S(1)}, f32[64,128]{1,0:T(8,128)}, u32[]{:S(2)}) copy-start(f32[64,128]{1,0:T(8,128)} %get-tuple-element.85) | copy-start | bytes 98308
  566.5 7.6 %collective-permute-start.8 = (f32[15,1,64,128]{3,2,0,1:T(8,128)S(1)}, f32[15,1,64,128]{3,2,0,1:T(8,128)S(1)}, u32[]{:S(2)}, u32[]{:S(2)}) collective-permute-start(f32[15,1,64,128]{3,2,0,1:T(8,128)S(1)} %get-tuple-element.34), channel_id=1, source_target_pairs={{32,0},{64,32},{96,64},{128,96},{160,128},{192,160},{224,192},{33,... | collective-permute-start | bytes 1474568 | tf_op jit(solution)/shard_map/ppermute | solution.py:30
  567.9 7.6 %collective-permute-start.9 = (f32[15,1,64,128]{3,2,0,1:T(8,128)S(1)}, f32[15,1,64,128]{3,2,0,1:T(8,128)S(1)}, u32[]{:S(2)}, u32[]{:S(2)}) collective-permute-start(f32[15,1,64,128]{3,2,0,1:T(8,128)S(1)} %get-tuple-element.34), channel_id=1, source_target_pairs={{0,32},{32,64},{64,96},{96,128},{128,160},{160,192},{192,224},{1,3... | collective-permute-start | bytes 1474568 | tf_op jit(solution)/shard_map/ppermute | solution.py:29
  576.5 60.5 %copy-start.3 = (f32[15,1,64,128]{3,2,1,0:T(8,128)S(1)}, f32[15,1,64,128]{3,2,1,0:T(8,128)}, u32[]{:S(2)}) copy-start(f32[15,1,64,128]{3,2,1,0:T(8,128)} %param.6) | copy-start | bytes 1474564
  (78 other events, 283.1 us)
where the time goes:
time: 649 us; the launch traced here: 639 us
  other arithmetic  266 us (41%)
  blocking collectives  165 us (25%)
  waiting for transfers between devices  107 us (16%)
  starting transfers between devices  52.3 us (8%)
  local copies, waits for them, and re-layouts  40.7 us (6%)
  between operations  7.29 us (1%)
    scatter-add x16, other arithmetic, couple_modes(): jax.ops.segment_sum(scaled * flattened[first_mode], second_mode, num_segm...  116 us
    scatter-add x16, other arithmetic, couple_modes(): jax.ops.segment_sum(scaled * flattened[second_mode], first_mode, num_segm...  113 us
    all_to_all x1, blocking collectives, operate(): lax.all_to_all(stacked, CHAOS, split_axis=3, concat_axis=1, tiled=True)  89.6 us
    all_to_all x1, waiting for transfers between devices, operate(): lax.all_to_all(stacked, CHAOS, split_axis=3, concat_axis=1, tiled=True)  84.7 us
    psum x4, blocking collectives, one_axis_at_a_time(): return functools.reduce(lax.psum, axes, x)  53.3 us
    ppermute x5, starting transfers between devices, padded(): before = lax.ppermute(last, axis, up)  24.8 us
    all_to_all x1, blocking collectives, operate(): lax.all_to_all(summed, CHAOS, split_axis=0, concat_axis=2, tiled=True)  22.5 us
    unnamed x244, local copies, waits for them, and re-layouts  19.9 us
  transfers between devices with their start and end apart: 12, of which 6 were waited for; matrix products, arithmetic and copies ran while one was open for 1% of the time, Pallas kernels for 0%

commit v1 on v0

v1 whole, which is shorter than its diff:
```python
import functools

import jax
import jax.numpy as jnp
from jax import lax
from jax.experimental import pallas as pl
from jax.experimental.pallas import tpu as pltpu
from jax.sharding import PartitionSpec as P

CENTER_BOUND = 1.05
HALF_WIDTH = 0.95
FIRST_COEF = 4.0 * CENTER_BOUND / (2.0 * CENTER_BOUND * CENTER_BOUND - HALF_WIDTH * HALF_WIDTH)
SECOND_COEF = 2.0 / (2.0 * CENTER_BOUND * CENTER_BOUND - HALF_WIDTH * HALF_WIDTH)
SLOT = 16
F32 = jnp.float32
BF16 = jnp.bfloat16
MESH = pl.DeviceIdType.MESH


def al(value, unit):
    return pl.multiple_of(value, unit)


def kernel(
    chaos_n, space_n, terms, own_modes, rows,
    v_ref, f_ref, cond_ref, lists_ref,
    sol_ref, res_ref, dir_ref,
    x0, x1, ft, q_ref, mq_ref, cy, cxm, cxp, c0m, c0p, oc, ob, kf, kb,
    gh, gl, oa, wh, wl, ph, plo, acc,
    t0, t1, hxm0, hxm1, hxp0, hxp1, hym0, hym1, hyp0, hyp1,
    y0, y1, o0, o1, z0, z1, zxm0, zxm1, zxp0, zxp1,
    dots, dsum, dga, dgb,
    coef_sem, send_sem, a2a_sem, fwd_sem, ret_sem, zx_sem, dota_sem, dotb_sem,
):
    me = lax.axis_index("chaos")
    sp = lax.axis_index("space")
    up = lax.rem(sp + 1, space_n)
    down = lax.rem(sp + space_n - 1, space_n)
    right = lax.rem(me + 1, chaos_n)
    left = lax.rem(me + chaos_n - 1, chaos_n)
    slots = chaos_n * SLOT
    flat = rows * SLOT
    width = v_ref.shape[-1]

    def peer(k):
        return lax.rem(me + k, chaos_n)

    def source(k):
        return lax.rem(me + chaos_n - k, chaos_n)

    def block(c):
        return pl.ds(al(c * 32, 32), 32)

    def remote(src, dst, ssem, rsem, target):
        return pltpu.make_async_remote_copy(
            src_ref=src, dst_ref=dst, send_sem=ssem, recv_sem=rsem,
            device_id=target, device_id_type=MESH,
        )

    def drain(ref, count, sem):
        pltpu.make_async_copy(ref.at[pl.ds(0, count)], ref.at[pl.ds(0, count)], sem).wait()

    barrier = pltpu.get_barrier_semaphore()

    def greet_chaos(k, carry):
        pl.semaphore_signal(barrier, inc=1, device_id={"chaos": peer(k)}, device_id_type=MESH)
        return carry

    lax.fori_loop(1, chaos_n, greet_chaos, 0)

    def greet_space(k, carry):
        pl.semaphore_signal(
            barrier, inc=1, device_id={"space": lax.rem(sp + k, space_n)}, device_id_type=MESH
        )
        return carry

    lax.fori_loop(1, space_n, greet_space, 0)

    tiles = rows // 8
    x0[...] = jnp.zeros_like(x0)
    ft[...] = jnp.zeros_like(ft)
    cy[...] = jnp.zeros_like(cy)

    def turn_in(m, carry):
        for tile in range(tiles):
            where = pl.ds(tile * 128 + m, 8, stride=SLOT)
            x0[where, :] = v_ref[m, pl.ds(tile * 8, 8), :]
            ft[where, :] = f_ref[m, pl.ds(tile * 8, 8), :]
        return carry

    lax.fori_loop(0, own_modes, turn_in, 0)
    for j in range(terms + 1):
        for tile in range(tiles):
            cy[pl.ds(tile * 128 + j, 8, stride=SLOT), :] = cond_ref[j, pl.ds(tile * 8, 8), :]

    pl.semaphore_wait(barrier, chaos_n - 1 + space_n - 1)

    coef_copies = (
        remote(cy.at[block(me)], cxm.at[pl.ds(0, 32)], send_sem.at[0], coef_sem.at[0], {"space": up}),
        remote(cy.at[block(me)], cxp.at[pl.ds(0, 32)], send_sem.at[1], coef_sem.at[1], {"space": down}),
        remote(cond_ref.at[0], c0m, send_sem.at[2], coef_sem.at[2], {"space": up}),
        remote(cond_ref.at[0], c0p, send_sem.at[3], coef_sem.at[3], {"space": down}),
    )
    for copy in coef_copies:
        copy.start()

    def send_block(src, dst, ssem, rsems, k):
        c = peer(k)
        remote(src.at[block(c)], dst.at[block(me)], ssem, rsems.at[k], {"chaos": c}).start()

    def send_all(src, dst, ssem, rsems):
        def body(k, carry):
            send_block(src, dst, ssem, rsems, k)
            return carry

        lax.fori_loop(1, chaos_n, body, 0)
        dst[block(me), :] = src[block(me), :]

    send_all(x0, t0, send_sem.at[4], a2a_sem.at[0])

    lane = lax.broadcasted_iota(jnp.int32, (1, width), 1)
    zm_mask = jnp.where(lane > 0, 0.5, 0.0).astype(F32)
    zp_mask = jnp.where(lane < width - 1, 0.5, 0.0).astype(F32)
    xm_mask = jnp.where(sp > 0, 0.5, 0.0).astype(F32)
    xp_mask = jnp.where(sp < space_n - 1, 0.5, 0.0).astype(F32)

    for copy in coef_copies:
        copy.wait()

    for r in range(2):
        y = me * 2 + r
        cn = cy[pl.ds(al(y * SLOT, SLOT), SLOT), :]
        cm = cy[pl.ds(al(lax.rem(y + rows - 1, rows) * SLOT, SLOT), SLOT), :]
        cp = cy[pl.ds(al(lax.rem(y + 1, rows) * SLOT, SLOT), SLOT), :]
        ym_mask = jnp.where(y > 0, 0.5, 0.0).astype(F32)
        yp_mask = jnp.where(y < rows - 1, 0.5, 0.0).astype(F32)
        total = 3.0 * cn
        around = (
            (cxm[pl.ds(r * SLOT, SLOT), :], xm_mask),
            (cxp[pl.ds(r * SLOT, SLOT), :], xp_mask),
            (cm, ym_mask),
            (cp, yp_mask),
            (pltpu.roll(cn, 1, 1), zm_mask),
            (pltpu.roll(cn, width - 1, 1), zp_mask),
        )
        for n, (other, mask) in enumerate(around):
            total = total + other * mask
            kf[pl.ds((r * 7 + n + 1) * SLOT, SLOT), :] = (cn + other) * mask
        kf[pl.ds(r * 7 * SLOT, SLOT), :] = total
    for r in range(2):
        for j in range(terms + 1):
            for n in range(7):
                row = kf[pl.ds((r * 7 + n) * SLOT + j, 1), :]
                kb[pl.ds(((r * (terms + 1) + j) * 7 + n) * 8, 8), :] = jnp.broadcast_to(row, (8, width))

    c0 = cond_ref[0]
    yrow = lax.broadcasted_iota(jnp.int32, (rows, 1), 0)
    around = (
        (c0m[...], xm_mask),
        (c0p[...], xp_mask),
        (pltpu.roll(c0, 1, 0), jnp.where(yrow > 0, 0.5, 0.0).astype(F32)),
        (pltpu.roll(c0, rows - 1, 0), jnp.where(yrow < rows - 1, 0.5, 0.0).astype(F32)),
        (pltpu.roll(c0, 1, 1), zm_mask),
        (pltpu.roll(c0, width - 1, 1), zp_mask),
    )
    diagonal = 3.0 * c0
    for other, mask in around:
        diagonal = diagonal + other * mask
    inverse = 1.0 / diagonal
    oc[6] = inverse
    for n, (other, mask) in enumerate(around):
        oc[n] = SECOND_COEF * ((c0 + other) * mask) * inverse

    def spread(tile, carry):
        for n in range(7):
            group = oc[n, pl.ds(al(tile * 8, 8), 8), :]
            for i in range(8):
                at = al((tile * 56 + i * 7 + n) * 8, 8)
                ob[pl.ds(at, 8), :] = jnp.broadcast_to(group[i : i + 1, :], (8, width))
        return carry

    lax.fori_loop(0, tiles, spread, 0)

    ts, hxms, hxps, hyms, hyps = ((t0, t1), (hxm0, hxm1), (hxp0, hxp1), (hym0, hym1), (hyp0, hyp1))
    ys, os, zs, zxms, zxps = ((y0, y1), (o0, o1), (z0, z1), (zxm0, zxm1), (zxp0, zxp1))

    def forward_block(it, k):
        c = source(k)
        t = ts[it]
        half = pl.ds(al(c * SLOT, SLOT), SLOT)
        rsem = fwd_sem.at[it].at[k]
        base = 8 + it * 8
        remote(t.at[block(c)], hxms[it].at[block(c)], send_sem.at[base], rsem, {"space": up}).start()
        remote(t.at[block(c)], hxps[it].at[block(c)], send_sem.at[base + 1], rsem, {"space": down}).start()
        low = t.at[pl.ds(al(c * 32, 32), SLOT)]
        high = t.at[pl.ds(al(c * 32 + SLOT, SLOT), SLOT)]
        kr = lax.rem(k + 1, chaos_n)
        kl = lax.rem(k + chaos_n - 1, chaos_n)
        remote(high, hyms[it].at[half], send_sem.at[base + 2], fwd_sem.at[it].at[kr], {"chaos": right}).start()
        remote(low, hyps[it].at[half], send_sem.at[base + 3], fwd_sem.at[it].at[kl], {"chaos": left}).start()

    def receive_forward(it, k):
        @pl.when(k > 0)
        def _():
            c = source(k)
            remote(
                ts[it].at[block(c)], ts[it].at[block(c)], send_sem.at[4], a2a_sem.at[it].at[k], {"chaos": left}
            ).wait_recv()

        forward_block(it, k)

    index = lax.broadcasted_iota(jnp.int32, (slots, lists_ref.shape[-1]), 0).astype(F32)
    nt = (((1,), (1,)), ((), ()))
    per = chaos_n // terms if chaos_n >= terms else 1

    def build(j, carry):
        first = lists_ref[pl.ds(j, 1), :]
        second = lists_ref[pl.ds(j + terms, 1), :]
        weight = lists_ref[pl.ds(j + 2 * terms, 1), :]
        weight_high = weight.astype(BF16).astype(F32)
        weight_low = weight - weight_high
        oa[...] = jnp.where(index == first, 1.0, 0.0).astype(BF16)
        here = index == second
        wh[...] = jnp.where(here, weight_high, 0.0).astype(BF16)
        wl[...] = jnp.where(here, weight_low, 0.0).astype(BF16)
        a, b, c = (oa[...], wh[...], wl[...])
        g = lax.dot_general(a, b, nt, preferred_element_type=F32)
        g = g + lax.dot_general(a, c, nt, preferred_element_type=F32)
        g = g + lax.dot_general(b, a, nt, preferred_element_type=F32)
        g = g + lax.dot_general(c, a, nt, preferred_element_type=F32)
        high = g.astype(BF16)
        gh[j] = high
        gl[j] = (g - high.astype(F32)).astype(BF16)

        if chaos_n >= terms:
            for n in range(per):
                receive_forward(0, j * per + n)
        return carry

    lax.fori_loop(0, terms, build, 0)
    if chaos_n < terms:
        for k in range(chaos_n):
            receive_forward(0, jnp.int32(k))

    def operate(it):
        t, hxm, hxp, hym, hyp, y, o = (ts[it], hxms[it], hxps[it], hyms[it], hyps[it], ys[it], os[it])

        def products(k, carry):
            c = source(k)
            drain_ref = hxm.at[pl.ds(0, 96)] if flat >= 96 else None
            pltpu.make_async_copy(drain_ref, drain_ref, fwd_sem.at[it].at[k]).wait()
            for r in range(2):
                for h in range(2):
                    at = pl.ds(al(c * 32 + r * SLOT + h * 8, 8), 8)
                    lo_at = pl.ds(al(c * 32 + h * 8, 8), 8)
                    hi_at = pl.ds(al(c * 32 + SLOT + h * 8, 8), 8)
                    half = pl.ds(al(c * SLOT + h * 8, 8), 8)
                    v = t[at, :]
                    near = (
                        v,
                        hxm[at, :],
                        hxp[at, :],
                        hym[half, :] if r == 0 else t[lo_at, :],
                        t[hi_at, :] if r == 0 else hyp[half, :],
                        pltpu.roll(v, 1, 1),
                        pltpu.roll(v, width - 1, 1),
                    )
                    for j in range(terms + 1):
                        base = (r * (terms + 1) + j) * 56
                        value = kb[pl.ds(base, 8), :] * near[0]
                        for n in range(1, 7):
                            value = value - kb[pl.ds(base + n * 8, 8), :] * near[n]
                        if j == 0:
                            y[at, :] = value
                        else:
                            acc[j - 1, pl.ds(h * 8, 8), :] = value
                for j in range(terms):
                    value = acc[j, pl.ds(0, SLOT), :]
                    high = value.astype(BF16)
                    to = pl.ds(al(c * SLOT, SLOT), SLOT)
                    ph[j, to, pl.ds(r * width, width)] = high
                    plo[j, to, pl.ds(r * width, width)] = (value - high.astype(F32)).astype(BF16)
            return carry

        lax.fori_loop(0, chaos_n, products, 0)

        step = min(slots, 256)
        for part in range(slots // step):
            lines = pl.ds(part * step, step)

            def mix(j, total):
                a, b = (gh[j, lines, :], ph[j])
                total = total + jnp.dot(a, b, preferred_element_type=F32)
                total = total + jnp.dot(a, plo[j], preferred_element_type=F32)
                return total + jnp.dot(gl[j, lines, :], b, preferred_element_type=F32)

            total = lax.fori_loop(0, terms, mix, jnp.zeros((step, 2 * width), F32))
            for c in range(step // SLOT):
                for r in range(2):
                    at = pl.ds(part * step * 2 + c * 32 + r * SLOT, SLOT)
                    y[at, :] = y[at, :] + total[c * SLOT : (c + 1) * SLOT, r * width : (r + 1) * width]
        send_all(y, o, send_sem.at[5 + it], ret_sem.at[it])

    def scaled_rows(it, k, carry):
        c = source(k)
        o, z = (os[it], zs[it])

        @pl.when(k > 0)
        def _():
            remote(o.at[block(c)], o.at[block(c)], send_sem.at[5], ret_sem.at[it].at[k], {"chaos": left}).wait_recv()

        for r in range(2):
            inv = ob[pl.ds(al((c * 2 + r) * 56 + 48, 8), 8), :]
            for h in range(2):
                at = pl.ds(al(c * 32 + r * SLOT + h * 8, 8), 8)
                value = o[at, :]
                if it == 0:
                    value = ft[at, :] - value
                    ft[at, :] = value
                else:
                    q_ref[at, :] = value
                z[at, :] = value * inv
        base = 12 + it * 8
        remote(z.at[block(c)], zxms[it].at[block(c)], send_sem.at[base], zx_sem.at[it].at[k], {"space": up}).start()
        remote(z.at[block(c)], zxps[it].at[block(c)], send_sem.at[base + 1], zx_sem.at[it].at[k], {"space": down}).start()
        return carry

    def precondition(it):
        z, zxm, zxp = (zs[it], zxms[it], zxps[it])
        lax.fori_loop(0, chaos_n, functools.partial(scaled_rows, it), 0)
        zero = jnp.zeros((8, width), F32)

        def finish(k, carry):
            c = source(k)
            sums = carry
            pltpu.make_async_copy(zxm.at[pl.ds(0, 64)], zxm.at[pl.ds(0, 64)], zx_sem.at[it].at[k]).wait()
            for r in range(2):
                line = c * 2 + r
                prev = lax.rem(line + rows - 1, rows)
                after = lax.rem(line + 1, rows)
                coef = [ob[pl.ds(al(line * 56 + n * 8, 8), 8), :] for n in range(6)]
                for h in range(2):
                    at = pl.ds(al(line * SLOT + h * 8, 8), 8)
                    v = z[at, :]
                    near = (
                        zxm[at, :],
                        zxp[at, :],
                        z[pl.ds(al(prev * SLOT + h * 8, 8), 8), :],
                        z[pl.ds(al(after * SLOT + h * 8, 8), 8), :],
                        pltpu.roll(v, 1, 1),
                        pltpu.roll(v, width - 1, 1),
                    )
                    value = (FIRST_COEF - SECOND_COEF) * v
                    for n in range(6):
                        value = value + coef[n] * near[n]
                    if it == 0:
                        x1[at, :] = value
                        sums = (sums[0] + ft[at, :] * value, sums[1])
                    else:
                        mq_ref[at, :] = value
                        image = q_ref[at, :]
                        sums = (sums[0] + x1[at, :] * image, sums[1] + image * value)
            if it == 0:
                @pl.when(k > 0)
                def _():
                    back = lax.rem(chaos_n - k, chaos_n)
                    remote(
                        x1.at[block(c)], t1.at[block(me)], send_sem.at[7], a2a_sem.at[1].at[back], {"chaos": c}
                    ).start()
            return sums

        return lax.fori_loop(0, chaos_n, finish, (zero, zero))

    operate(0)
    energy, _ = precondition(0)
    t1[block(me), :] = x1[block(me), :]

    def take(k, carry):
        receive_forward(1, k)
        return carry

    lax.fori_loop(0, chaos_n, take, 0)
    operate(1)
    curve, image = precondition(1)

    dots[...] = jnp.zeros_like(dots)
    for n, value in enumerate((energy, curve, image)):
        dots[pl.ds(n, 1), :] = jnp.sum(value, axis=0, keepdims=True)

    def tell(k, carry):
        remote(dots, dga.at[k], send_sem.at[24], dota_sem.at[k], {"chaos": peer(k)}).start()
        return carry

    lax.fori_loop(1, chaos_n, tell, 0)

    def hear(k, total):
        remote(dots, dga.at[k], send_sem.at[24], dota_sem.at[k], {"chaos": left}).wait_recv()
        return total + dga[k]

    dsum[...] = lax.fori_loop(1, chaos_n, hear, dots[...])

    def tell_space(k, carry):
        there = lax.rem(sp + k, space_n)
        remote(dsum, dgb.at[k], send_sem.at[25], dotb_sem.at[k], {"space": there}).start()
        return carry

    lax.fori_loop(1, space_n, tell_space, 0)

    def hear_space(k, total):
        remote(dsum, dgb.at[k], send_sem.at[25], dotb_sem.at[k], {"space": up}).wait_recv()
        return total + dgb[k]

    sums = lax.fori_loop(1, space_n, hear_space, dsum[...])
    lanes = jnp.sum(sums, axis=1, keepdims=True)
    energy_start, curvature, image_energy = (lanes[0:1, :], lanes[1:2, :], lanes[2:3, :])
    step_size = energy_start / curvature
    energy_next = energy_start - 2.0 * step_size * curvature + step_size * step_size * image_energy
    ratio = 1.0 + energy_next / energy_start
    step_all = jnp.broadcast_to(step_size, (8, width))
    ratio_all = jnp.broadcast_to(ratio, (8, width))

    def turn_out(m, carry):
        for tile in range(tiles):
            where = pl.ds(tile * 128 + m, 8, stride=SLOT)
            there = pl.ds(tile * 8, 8)
            search = x1[where, :]
            sol_ref[m, there, :] = v_ref[m, there, :] + step_all * search
            res_ref[m, there, :] = ft[where, :] - step_all * q_ref[where, :]
            dir_ref[m, there, :] = ratio_all * search - step_all * mq_ref[where, :]
        return carry

    lax.fori_loop(0, own_modes, turn_out, 0)

    others = chaos_n - 1
    drain(x0, others * 32, send_sem.at[4])
    drain(x1, others * 32, send_sem.at[7])
    for it in range(2):
        drain(ys[it], others * 32, send_sem.at[5 + it])
        for n in range(2):
            drain(ts[it], flat, send_sem.at[8 + it * 8 + n])
            drain(ts[it], flat // 2, send_sem.at[10 + it * 8 + n])
            drain(zs[it], flat, send_sem.at[12 + it * 8 + n])
    pltpu.make_async_copy(dga.at[pl.ds(1, chaos_n - 1)], dga.at[pl.ds(1, chaos_n - 1)], send_sem.at[24]).wait()
    pltpu.make_async_copy(dgb.at[pl.ds(1, space_n - 1)], dgb.at[pl.ds(1, space_n - 1)], send_sem.at[25]).wait()


def per_device(chaos_n, space_n, source_term, start_field, conductivity, pair_modes, pair_weight):
    own_modes, _, rows, width = source_term.shape
    terms, pairs = pair_weight.shape
    slots = chaos_n * SLOT
    flat = rows * SLOT
    padded = -(-pairs // 128) * 128
    ends = pair_modes + pair_modes // own_modes * (SLOT - own_modes)
    lists = jnp.concatenate(
        [ends[:, :, 0].astype(F32), ends[:, :, 1].astype(F32), pair_weight], axis=0
    )
    lists = jnp.pad(lists, ((0, 0), (0, padded - pairs)), constant_values=-1.0)
    field = pltpu.VMEM((flat, width), F32)
    half = pltpu.VMEM((flat // 2, width), F32)
    vmem = pl.BlockSpec(memory_space=pltpu.VMEM)
    shape = jax.ShapeDtypeStruct((own_modes, rows, width), F32)
    outs = pl.pallas_call(
        functools.partial(kernel, chaos_n, space_n, terms, own_modes, rows),
        out_shape=(shape, shape, shape),
        in_specs=[vmem] * 4,
        out_specs=(vmem, vmem, vmem),
        scratch_shapes=[field] * 6
        + [pltpu.VMEM((32, width), F32)] * 2
        + [pltpu.VMEM((rows, width), F32)] * 2
        + [
            pltpu.VMEM((7, rows, width), F32),
            pltpu.VMEM((rows * 56, width), F32),
            pltpu.VMEM((14 * SLOT, width), F32),
            pltpu.VMEM((2 * (terms + 1) * 56, width), F32),
            pltpu.VMEM((terms, slots, slots), BF16),
            pltpu.VMEM((terms, slots, slots), BF16),
            pltpu.VMEM((slots, padded), BF16),
            pltpu.VMEM((slots, padded), BF16),
            pltpu.VMEM((slots, padded), BF16),
            pltpu.VMEM((terms, slots, 2 * width), BF16),
            pltpu.VMEM((terms, slots, 2 * width), BF16),
            pltpu.VMEM((terms, SLOT, width), F32),
        ]
        + [field] * 6
        + [half] * 4
        + [field] * 10
        + [
            pltpu.VMEM((8, width), F32),
            pltpu.VMEM((8, width), F32),
            pltpu.VMEM((chaos_n, 8, width), F32),
            pltpu.VMEM((space_n, 8, width), F32),
            pltpu.SemaphoreType.DMA((4,)),
            pltpu.SemaphoreType.DMA((26,)),
            pltpu.SemaphoreType.DMA((2, chaos_n)),
            pltpu.SemaphoreType.DMA((2, chaos_n)),
            pltpu.SemaphoreType.DMA((2, chaos_n)),
            pltpu.SemaphoreType.DMA((2, chaos_n)),
            pltpu.SemaphoreType.DMA((chaos_n,)),
            pltpu.SemaphoreType.DMA((space_n,)),
        ],
        compiler_params=pltpu.CompilerParams(
            collective_id=0, has_side_effects=True, vmem_limit_bytes=60 * 1024 * 1024
        ),
    )(
        start_field.reshape(own_modes, rows, width),
        source_term.reshape(own_modes, rows, width),
        conductivity.reshape(terms + 1, rows, width),
        lists,
    )
    return tuple(out.reshape(source_term.shape) for out in outs)


def solution(mesh):
    chaos_n, space_n = (mesh.shape["chaos"], mesh.shape["space"])
    field = P("chaos", "space", None, None)
    return jax.shard_map(
        functools.partial(per_device, chaos_n, space_n),
        mesh=mesh,
        in_specs=(field, field, P(None, "space", None, None), P(), P()),
        out_specs=(field, field, field),
        check_vma=False,
    )
```

time: 649 us -> 134 us (0.21)
  the two profiles are of different devices: /device:TPU:32 before, /device:TPU:1 now
where the time goes in v1:
time: 134 us
  Pallas kernels  128 us (96%)
  local copies, waits for them, and re-layouts  4.6 us (3%)
  other arithmetic  1.42 us (1%)
    pallas_call x1, Pallas kernels, per_device(): pl.pallas_call(functools.partial(kernel, chaos_n, space_n, terms, own_mod...  128 us
    unnamed x9, local copies, waits for them, and re-layouts  4.6 us

profile of v1, /device:TPU:1, one launch (start us, length us, event | category | flops | bytes accessed | tf_op | source)
XLA Modules:
  0.0 134.2 jit_solution(16663507220136935691)
XLA Ops:
  0.6 0.8 fusion
  1.4 0.0 copy-start.2
  1.4 0.7 copy-done.2
  2.1 0.6 select_maximum_fusion.lists_ref
  2.8 127.5 %shard_map.76 = (f32[15,64,128]{2,1,0:T(8,128)}, f32[15,64,128]{2,1,0:T(8,128)}, f32[15,64,128]{2,1,0:T(8,128)}) custom-call(f32[15,64,128]{2,1,0:T(8,128)} %bitcast.19, f32[15,64,128]{2,1,0:T(8,128)} %bitcast.20, f32[9,64,128]{2,1,0:T(8,128)} %bitcast.21, f32[24,512]{1,0:T(8,128)} %select_maximum_fusion.lists_ref), custom_call_target="tpu_custom_call" | custom-call | tf_op jit(solution)/shard_map/pallas_call | solution.py:462
  130.3 0.0 copy-start.1
  130.3 1.9 %copy.19 = f32[15,1,64,128]{3,2,1,0:T(8,128)} copy(f32[15,1,64,128]{3,2,1,0:T(8,128)} %bitcast.18) | data formatting | bytes 983040
  132.2 0.0 copy-done.1
  132.2 0.0 copy-start
  132.2 0.8 copy.20
  133.0 0.4 copy-done
  133.4 0.8 copy.21
  (1 shorter events, 0.0 us)
Async XLA Ops:
  1.4 0.7 copy-start.2
  130.3 1.9 %copy-start.1 = (f32[15,64,128]{2,1,0:T(8,128)S(1)}, f32[15,64,128]{2,1,0:T(8,128)}, u32[]{:S(2)}) copy-start(f32[15,64,128]{2,1,0:T(8,128)} %get-tuple-element.7) | copy-start | bytes 1474564
  132.2 1.2 copy-start

commit v2 on v1

v2 whole, which is shorter than its diff:
```python
import functools

import jax
import jax.numpy as jnp
from jax import lax
from jax.experimental import pallas as pl
from jax.experimental.pallas import tpu as pltpu
from jax.sharding import PartitionSpec as P

CENTER_BOUND = 1.05
HALF_WIDTH = 0.95
FIRST_COEF = 4.0 * CENTER_BOUND / (2.0 * CENTER_BOUND * CENTER_BOUND - HALF_WIDTH * HALF_WIDTH)
SECOND_COEF = 2.0 / (2.0 * CENTER_BOUND * CENTER_BOUND - HALF_WIDTH * HALF_WIDTH)
SLOT = 16
F32 = jnp.float32
BF16 = jnp.bfloat16
MESH = pl.DeviceIdType.MESH


def al(value, unit):
    return pl.multiple_of(value, unit)


def kernel(
    chaos_n, space_n, terms, own_modes, rows,
    v_ref, f_ref, cond_ref, lists_ref,
    sol_ref, res_ref, dir_ref,
    xv, xf, rr, ss, qq, mq, zr, zrm, zrp, zq, zqm, zqp,
    tv, tf, tr, tz, ts, tw, y0, y1,
    vxm, vxp, zxm, zxp, sxm, sxp, wxm, wxp,
    vym, vyp, zym, zyp, sym, syp, wym, wyp,
    cy, cxm, cxp, c0m, c0p, oc, ob, kf, kb, tb,
    gh, gl, oa, wh, wl, ph, plo, acc,
    sums, dots, dsum, dga, dgb,
    coef_sem, send_sem, a2a_sem, halo_sem, slab_sem, dota_sem, dotb_sem,
):
    me = lax.axis_index("chaos")
    sp = lax.axis_index("space")
    up = lax.rem(sp + 1, space_n)
    down = lax.rem(sp + space_n - 1, space_n)
    right = lax.rem(me + 1, chaos_n)
    left = lax.rem(me + chaos_n - 1, chaos_n)
    slots = chaos_n * SLOT
    flat = rows * SLOT
    width = v_ref.shape[-1]
    tiles = rows // 8
    per = -(-chaos_n // (terms // 2))
    lag = max(2, chaos_n // 4)

    def swing(i):
        return (2 * lax.rem(i, 2) - 1) * ((i + 1) // 2)

    def target(i):
        return lax.rem(me + chaos_n + swing(i), chaos_n)

    def source(i):
        return lax.rem(me + chaos_n - swing(i), chaos_n)

    def block(c):
        return pl.ds(al(c * 32, 32), 32)

    def low(c):
        return pl.ds(al(c * 32, 32), SLOT)

    def high(c):
        return pl.ds(al(c * 32 + SLOT, SLOT), SLOT)

    def half(c):
        return pl.ds(al(c * SLOT, SLOT), SLOT)

    def remote(src, dst, ssem, rsem, device):
        return pltpu.make_async_remote_copy(
            src_ref=src, dst_ref=dst, send_sem=ssem, recv_sem=rsem,
            device_id=device, device_id_type=MESH,
        )

    def drain(ref, count, sem):
        pltpu.make_async_copy(ref.at[pl.ds(0, count)], ref.at[pl.ds(0, count)], sem).wait()

    barrier = pltpu.get_barrier_semaphore()

    def greet_chaos(k, carry):
        pl.semaphore_signal(
            barrier, inc=1, device_id={"chaos": lax.rem(me + k, chaos_n)}, device_id_type=MESH
        )
        return carry

    lax.fori_loop(1, chaos_n, greet_chaos, 0)

    def greet_space(k, carry):
        pl.semaphore_signal(
            barrier, inc=1, device_id={"space": lax.rem(sp + k, space_n)}, device_id_type=MESH
        )
        return carry

    lax.fori_loop(1, space_n, greet_space, 0)

    blank = jnp.zeros((8, width), F32)

    def turn_in(from_ref, to_ref):
        def body(m, carry):
            for tile in range(tiles):
                to_ref[pl.ds(tile * 128 + m, 8, stride=SLOT), :] = from_ref[m, pl.ds(tile * 8, 8), :]
            return carry

        lax.fori_loop(0, own_modes, body, 0)
        for m in range(own_modes, SLOT):
            for tile in range(tiles):
                to_ref[pl.ds(tile * 128 + m, 8, stride=SLOT), :] = blank

    turn_in(v_ref, xv)
    for j in range(SLOT):
        for tile in range(tiles):
            value = cond_ref[j, pl.ds(tile * 8, 8), :] if j <= terms else blank
            cy[pl.ds(tile * 128 + j, 8, stride=SLOT), :] = value

    pl.semaphore_wait(barrier, chaos_n - 1 + space_n - 1)

    coef_copies = (
        remote(cy.at[block(me)], cxm.at[pl.ds(0, 32)], send_sem.at[0], coef_sem.at[0], {"space": up}),
        remote(cy.at[block(me)], cxp.at[pl.ds(0, 32)], send_sem.at[1], coef_sem.at[1], {"space": down}),
        remote(cond_ref.at[0], c0m, send_sem.at[2], coef_sem.at[2], {"space": up}),
        remote(cond_ref.at[0], c0p, send_sem.at[3], coef_sem.at[3], {"space": down}),
    )
    for copy in coef_copies:
        copy.start()

    def scatter(src, dst, which):
        def body(i, carry):
            c = target(i)
            remote(
                src.at[block(c)], dst.at[block(me)], send_sem.at[4 + which], a2a_sem.at[which].at[me], {"chaos": c}
            ).start()
            return carry

        lax.fori_loop(1, chaos_n, body, 0)
        dst[block(me), :] = src[block(me), :]

    def arrived(dst, which, i):
        @pl.when(i > 0)
        def _():
            c = source(i)
            remote(
                dst.at[block(c)], dst.at[block(c)], send_sem.at[4], a2a_sem.at[which].at[c], {"chaos": left}
            ).wait_recv()

    def spread_halo(src, halo, which, i):
        c = source(i)
        xm, xp, ym, yp = halo
        rsem = halo_sem.at[which].at[c]
        base = 8 + which * 4
        remote(src.at[block(c)], xm.at[block(c)], send_sem.at[base], rsem, {"space": up}).start()
        remote(src.at[block(c)], xp.at[block(c)], send_sem.at[base + 1], rsem, {"space": down}).start()
        remote(src.at[high(c)], ym.at[half(c)], send_sem.at[base + 2], rsem, {"chaos": right}).start()
        remote(src.at[low(c)], yp.at[half(c)], send_sem.at[base + 3], rsem, {"chaos": left}).start()

    def halo_arrived(which, i):
        c = source(i)
        pltpu.make_async_copy(xv.at[pl.ds(0, 96)], xv.at[pl.ds(0, 96)], halo_sem.at[which].at[c]).wait()

    def around(src, halo, c, r, h):
        xm, xp, ym, yp = halo
        at = pl.ds(al(c * 32 + r * SLOT + h * 8, 8), 8)
        other = pl.ds(al(c * 32 + (1 - r) * SLOT + h * 8, 8), 8)
        side = pl.ds(al(c * SLOT + h * 8, 8), 8)
        v = src[at, :]
        return (
            v,
            xm[at, :],
            xp[at, :],
            ym[side, :] if r == 0 else src[other, :],
            src[other, :] if r == 0 else yp[side, :],
            pltpu.roll(v, 1, 1),
            pltpu.roll(v, width - 1, 1),
        )

    scatter(xv, tv, 0)
    turn_in(f_ref, xf)
    scatter(xf, tf, 1)

    lane = lax.broadcasted_iota(jnp.int32, (1, width), 1)
    zm_mask = jnp.where(lane > 0, 0.5, 0.0).astype(F32)
    zp_mask = jnp.where(lane < width - 1, 0.5, 0.0).astype(F32)
    xm_mask = jnp.where(sp > 0, 0.5, 0.0).astype(F32)
    xp_mask = jnp.where(sp < space_n - 1, 0.5, 0.0).astype(F32)

    for copy in coef_copies:
        copy.wait()

    for r in range(2):
        y = me * 2 + r
        cn = cy[pl.ds(al(y * SLOT, SLOT), SLOT), :]
        cm = cy[pl.ds(al(lax.rem(y + rows - 1, rows) * SLOT, SLOT), SLOT), :]
        cp = cy[pl.ds(al(lax.rem(y + 1, rows) * SLOT, SLOT), SLOT), :]
        ym_mask = jnp.where(y > 0, 0.5, 0.0).astype(F32)
        yp_mask = jnp.where(y < rows - 1, 0.5, 0.0).astype(F32)
        total = 3.0 * cn
        near = (
            (cxm[pl.ds(r * SLOT, SLOT), :], xm_mask),
            (cxp[pl.ds(r * SLOT, SLOT), :], xp_mask),
            (cm, ym_mask),
            (cp, yp_mask),
            (pltpu.roll(cn, 1, 1), zm_mask),
            (pltpu.roll(cn, width - 1, 1), zp_mask),
        )
        for n, (other, mask) in enumerate(near):
            total = total + other * mask
            kf[pl.ds((r * 7 + n + 1) * SLOT, SLOT), :] = (cn + other) * mask
        kf[pl.ds(r * 7 * SLOT, SLOT), :] = total
    for r in range(2):
        for j in range(terms + 1):
            for n in range(7):
                row = kf[pl.ds((r * 7 + n) * SLOT + j, 1), :]
                kb[pl.ds(((r * (terms + 1) + j) * 7 + n) * 8, 8), :] = jnp.broadcast_to(row, (8, width))
        inv = 1.0 / kf[pl.ds(r * 7 * SLOT, 1), :]
        tb[pl.ds(r * 56 + 48, 8), :] = jnp.broadcast_to(inv, (8, width))
        for n in range(6):
            row = SECOND_COEF * kf[pl.ds((r * 7 + n + 1) * SLOT, 1), :] * inv
            tb[pl.ds(r * 56 + n * 8, 8), :] = jnp.broadcast_to(row, (8, width))

    c0 = cond_ref[0]
    yrow = lax.broadcasted_iota(jnp.int32, (rows, 1), 0)
    near = (
        (c0m[...], xm_mask),
        (c0p[...], xp_mask),
        (pltpu.roll(c0, 1, 0), jnp.where(yrow > 0, 0.5, 0.0).astype(F32)),
        (pltpu.roll(c0, rows - 1, 0), jnp.where(yrow < rows - 1, 0.5, 0.0).astype(F32)),
        (pltpu.roll(c0, 1, 1), zm_mask),
        (pltpu.roll(c0, width - 1, 1), zp_mask),
    )
    diagonal = 3.0 * c0
    for other, mask in near:
        diagonal = diagonal + other * mask
    inverse = 1.0 / diagonal
    oc[6] = inverse
    for n, (other, mask) in enumerate(near):
        oc[n] = SECOND_COEF * ((c0 + other) * mask) * inverse

    def spread(tile, carry):
        for n in range(7):
            group = oc[n, pl.ds(al(tile * 8, 8), 8), :]
            for i in range(8):
                at = al((tile * 56 + i * 7 + n) * 8, 8)
                ob[pl.ds(at, 8), :] = jnp.broadcast_to(group[i : i + 1, :], (8, width))
        return carry

    lax.fori_loop(0, tiles, spread, 0)

    def products(src, halo, which, y, i):
        halo_arrived(which, i)
        c = source(i)
        to = half(c)
        for r in range(2):
            for h in range(2):
                near = around(src, halo, c, r, h)
                for j in range(terms + 1):
                    base = (r * (terms + 1) + j) * 56
                    value = kb[pl.ds(base, 8), :] * near[0]
                    for n in range(1, 7):
                        value = value - kb[pl.ds(base + n * 8, 8), :] * near[n]
                    if j == 0:
                        y[pl.ds(al(c * 32 + r * SLOT + h * 8, 8), 8), :] = value
                    else:
                        acc[j - 1, pl.ds(h * 8, 8), :] = value
            for j in range(terms):
                value = acc[j, pl.ds(0, SLOT), :]
                top = value.astype(BF16)
                ph[j, to, pl.ds(r * width, width)] = top
                plo[j, to, pl.ds(r * width, width)] = (value - top.astype(F32)).astype(BF16)

    def mix(y):
        def body(j, total):
            a, b = (gh[j], ph[j])
            total = total + jnp.dot(a, b, preferred_element_type=F32)
            total = total + jnp.dot(a, plo[j], preferred_element_type=F32)
            return total + jnp.dot(gl[j], b, preferred_element_type=F32)

        total = lax.fori_loop(0, terms, body, jnp.zeros((slots, 2 * width), F32))
        for c in range(chaos_n):
            for r in range(2):
                at = pl.ds(c * 32 + r * SLOT, SLOT)
                y[at, :] = y[at, :] + total[c * SLOT : (c + 1) * SLOT, r * width : (r + 1) * width]

    index = lax.broadcasted_iota(jnp.int32, (slots, lists_ref.shape[-1]), 0).astype(F32)
    nt = (((1,), (1,)), ((), ()))

    def build(j, carry):
        first = lists_ref[pl.ds(j, 1), :]
        second = lists_ref[pl.ds(j + terms, 1), :]
        weight = lists_ref[pl.ds(j + 2 * terms, 1), :]
        weight_high = weight.astype(BF16).astype(F32)
        weight_low = weight - weight_high
        oa[...] = jnp.where(index == first, 1.0, 0.0).astype(BF16)
        here = index == second
        wh[...] = jnp.where(here, weight_high, 0.0).astype(BF16)
        wl[...] = jnp.where(here, weight_low, 0.0).astype(BF16)
        a, b, c = (oa[...], wh[...], wl[...])
        g = lax.dot_general(a, b, nt, preferred_element_type=F32)
        g = g + lax.dot_general(a, c, nt, preferred_element_type=F32)
        g = g + lax.dot_general(b, a, nt, preferred_element_type=F32)
        g = g + lax.dot_general(c, a, nt, preferred_element_type=F32)
        top = g.astype(BF16)
        gh[j] = top
        gl[j] = (g - top.astype(F32)).astype(BF16)

        def step(n, inner):
            i = (j - terms // 2) * per + n

            @pl.when(i >= 0)
            def _():
                arrived(tv, 0, i)
                spread_halo(tv, (vxm, vxp, vym, vyp), 0, i)

            @pl.when(i >= lag)
            def _():
                products(tv, (vxm, vxp, vym, vyp), 0, y0, i - lag)

            return inner

        return lax.fori_loop(0, per, step, carry)

    lax.fori_loop(0, terms, build, 0)

    def rest(i, carry):
        products(tv, (vxm, vxp, vym, vyp), 0, y0, i)
        return carry

    lax.fori_loop(chaos_n - lag, chaos_n, rest, 0)
    mix(y0)

    sums[...] = jnp.zeros_like(sums)

    def weigh(row, value):
        sums[pl.ds(row * 8, 8), :] = sums[pl.ds(row * 8, 8), :] + value

    def residual_step(i):
        arrived(tf, 1, i)
        c = source(i)
        for r in range(2):
            inv = tb[pl.ds(r * 56 + 48, 8), :]
            for h in range(2):
                at = pl.ds(al(c * 32 + r * SLOT + h * 8, 8), 8)
                value = tf[at, :] - y0[at, :]
                tr[at, :] = value
                tz[at, :] = value * inv
        spread_halo(tz, (zxm, zxp, zym, zyp), 1, i)

        @pl.when(i > 0)
        def _():
            remote(
                tr.at[block(c)], rr.at[block(me)], send_sem.at[6], a2a_sem.at[2].at[me], {"chaos": c}
            ).start()

    def search_step(i):
        halo_arrived(1, i)
        c = source(i)
        for r in range(2):
            coef = [tb[pl.ds(r * 56 + n * 8, 8), :] for n in range(6)]
            for h in range(2):
                at = pl.ds(al(c * 32 + r * SLOT + h * 8, 8), 8)
                near = around(tz, (zxm, zxp, zym, zyp), c, r, h)
                value = (FIRST_COEF - SECOND_COEF) * near[0]
                for n in range(6):
                    value = value + coef[n] * near[n + 1]
                ts[at, :] = value
                weigh(0, value * tr[at, :])
        spread_halo(ts, (sxm, sxp, sym, syp), 2, i)

    def chain(i, carry):
        @pl.when(i < chaos_n)
        def _():
            residual_step(i)

        @pl.when((i >= lag) & (i < chaos_n + lag))
        def _():
            search_step(i - lag)

        @pl.when(i >= 2 * lag)
        def _():
            products(ts, (sxm, sxp, sym, syp), 2, y1, i - 2 * lag)

        return carry

    lax.fori_loop(0, chaos_n + 2 * lag, chain, 0)
    rr[block(me), :] = tr[block(me), :]
    mix(y1)
    scatter(y1, qq, 3)

    def image_step(i, carry):
        c = source(i)
        for r in range(2):
            inv = tb[pl.ds(r * 56 + 48, 8), :]
            for h in range(2):
                at = pl.ds(al(c * 32 + r * SLOT + h * 8, 8), 8)
                tw[at, :] = y1[at, :] * inv
        spread_halo(tw, (wxm, wxp, wym, wyp), 3, i)
        return carry

    lax.fori_loop(0, chaos_n, image_step, 0)

    def slab_step(src, which, z, zm, zp, base, number):
        def body(i, carry):
            arrived(src, which, i)
            c = source(i)
            for r in range(2):
                inv = ob[pl.ds(al((c * 2 + r) * 56 + 48, 8), 8), :]
                for h in range(2):
                    at = pl.ds(al(c * 32 + r * SLOT + h * 8, 8), 8)
                    z[at, :] = src[at, :] * inv
            rsem = slab_sem.at[number].at[c]
            remote(z.at[block(c)], zm.at[block(c)], send_sem.at[base], rsem, {"space": up}).start()
            remote(z.at[block(c)], zp.at[block(c)], send_sem.at[base + 1], rsem, {"space": down}).start()
            return carry

        lax.fori_loop(0, chaos_n, body, 0)

    def slab_finish(z, zm, zp, number, to):
        def body(i, carry):
            c = source(i)
            pltpu.make_async_copy(xv.at[pl.ds(0, 64)], xv.at[pl.ds(0, 64)], slab_sem.at[number].at[c]).wait()
            for r in range(2):
                line = c * 2 + r
                prev = lax.rem(line + rows - 1, rows)
                after = lax.rem(line + 1, rows)
                coef = [ob[pl.ds(al(line * 56 + n * 8, 8), 8), :] for n in range(6)]
                for h in range(2):
                    at = pl.ds(al(line * SLOT + h * 8, 8), 8)
                    v = z[at, :]
                    near = (
                        zm[at, :],
                        zp[at, :],
                        z[pl.ds(al(prev * SLOT + h * 8, 8), 8), :],
                        z[pl.ds(al(after * SLOT + h * 8, 8), 8), :],
                        pltpu.roll(v, 1, 1),
                        pltpu.roll(v, width - 1, 1),
                    )
                    value = (FIRST_COEF - SECOND_COEF) * v
                    for n in range(6):
                        value = value + coef[n] * near[n]
                    to[at, :] = value
            return carry

        lax.fori_loop(0, chaos_n, body, 0)

    slab_step(rr, 2, zr, zrm, zrp, 24, 0)

    def image_dot(i, carry):
        halo_arrived(3, i)
        c = source(i)
        for r in range(2):
            coef = [tb[pl.ds(r * 56 + n * 8, 8), :] for n in range(6)]
            for h in range(2):
                at = pl.ds(al(c * 32 + r * SLOT + h * 8, 8), 8)
                near = around(tw, (wxm, wxp, wym, wyp), c, r, h)
                value = (FIRST_COEF - SECOND_COEF) * near[0]
                for n in range(6):
                    value = value + coef[n] * near[n + 1]
                image = y1[at, :]
                weigh(1, image * ts[at, :])
                weigh(2, image * value)
        return carry

    lax.fori_loop(0, chaos_n, image_dot, 0)
    dots[...] = blank
    for n in range(3):
        dots[pl.ds(n, 1), :] = jnp.sum(sums[pl.ds(n * 8, 8), :], axis=0, keepdims=True)

    def tell(k, carry):
        c = lax.rem(me + k, chaos_n)
        remote(dots, dga.at[k], send_sem.at[28], dota_sem.at[k], {"chaos": c}).start()
        return carry

    lax.fori_loop(1, chaos_n, tell, 0)

    slab_finish(zr, zrm, zrp, 0, ss)

    def hear(k, total):
        remote(dots, dga.at[k], send_sem.at[28], dota_sem.at[k], {"chaos": left}).wait_recv()
        return total + dga[k]

    dsum[...] = lax.fori_loop(1, chaos_n, hear, dots[...])

    def tell_space(k, carry):
        there = lax.rem(sp + k, space_n)
        remote(dsum, dgb.at[k], send_sem.at[29], dotb_sem.at[k], {"space": there}).start()
        return carry

    lax.fori_loop(1, space_n, tell_space, 0)

    slab_step(qq, 3, zq, zqm, zqp, 26, 1)
    slab_finish(zq, zqm, zqp, 1, mq)

    def hear_space(k, total):
        remote(dsum, dgb.at[k], send_sem.at[29], dotb_sem.at[k], {"space": up}).wait_recv()
        return total + dgb[k]

    whole = lax.fori_loop(1, space_n, hear_space, dsum[...])
    lanes = jnp.sum(whole, axis=1, keepdims=True)
    energy_start, curvature, image_energy = (lanes[0:1, :], lanes[1:2, :], lanes[2:3, :])
    step_size = energy_start / curvature
    energy_next = energy_start - 2.0 * step_size * curvature + step_size * step_size * image_energy
    ratio = 1.0 + energy_next / energy_start
    step_all = jnp.broadcast_to(step_size, (8, width))
    ratio_all = jnp.broadcast_to(ratio, (8, width))

    def turn_out(m, carry):
        for tile in range(tiles):
            where = pl.ds(tile * 128 + m, 8, stride=SLOT)
            there = pl.ds(tile * 8, 8)
            search = ss[where, :]
            sol_ref[m, there, :] = v_ref[m, there, :] + step_all * search
            res_ref[m, there, :] = rr[where, :] - step_all * qq[where, :]
            dir_ref[m, there, :] = ratio_all * search - step_all * mq[where, :]
        return carry

    lax.fori_loop(0, own_modes, turn_out, 0)

    for n, ref in enumerate((xv, xf, tr, y1)):
        drain(ref, (chaos_n - 1) * 32, send_sem.at[4 + n])
    for n, ref in enumerate((tv, tz, ts, tw)):
        for m, count in enumerate((flat, flat, flat // 2, flat // 2)):
            drain(ref, count, send_sem.at[8 + n * 4 + m])
    for n, ref in enumerate((zr, zq)):
        for m in range(2):
            drain(ref, flat, send_sem.at[24 + n * 2 + m])
    pltpu.make_async_copy(dga.at[pl.ds(1, chaos_n - 1)], dga.at[pl.ds(1, chaos_n - 1)], send_sem.at[28]).wait()
    pltpu.make_async_copy(dgb.at[pl.ds(1, space_n - 1)], dgb.at[pl.ds(1, space_n - 1)], send_sem.at[29]).wait()


def per_device(chaos_n, space_n, source_term, start_field, conductivity, pair_modes, pair_weight):
    own_modes, _, rows, width = source_term.shape
    terms, pairs = pair_weight.shape
    slots = chaos_n * SLOT
    flat = rows * SLOT
    padded = -(-pairs // 128) * 128
    ends = pair_modes + pair_modes // own_modes * (SLOT - own_modes)
    lists = jnp.concatenate(
        [ends[:, :, 0].astype(F32), ends[:, :, 1].astype(F32), pair_weight], axis=0
    )
    lists = jnp.pad(lists, ((0, 0), (0, padded - pairs)), constant_values=-1.0)
    field = pltpu.VMEM((flat, width), F32)
    half = pltpu.VMEM((flat // 2, width), F32)
    vmem = pl.BlockSpec(memory_space=pltpu.VMEM)
    shape = jax.ShapeDtypeStruct((own_modes, rows, width), F32)
    outs = pl.pallas_call(
        functools.partial(kernel, chaos_n, space_n, terms, own_modes, rows),
        out_shape=(shape, shape, shape),
        in_specs=[vmem] * 4,
        out_specs=(vmem, vmem, vmem),
        scratch_shapes=[field] * 28
        + [half] * 8
        + [field]
        + [pltpu.VMEM((32, width), F32)] * 2
        + [pltpu.VMEM((rows, width), F32)] * 2
        + [
            pltpu.VMEM((7, rows, width), F32),
            pltpu.VMEM((rows * 56, width), F32),
            pltpu.VMEM((14 * SLOT, width), F32),
            pltpu.VMEM((2 * (terms + 1) * 56, width), F32),
            pltpu.VMEM((112, width), F32),
            pltpu.VMEM((terms, slots, slots), BF16),
            pltpu.VMEM((terms, slots, slots), BF16),
            pltpu.VMEM((slots, padded), BF16),
            pltpu.VMEM((slots, padded), BF16),
            pltpu.VMEM((slots, padded), BF16),
            pltpu.VMEM((terms, slots, 2 * width), BF16),
            pltpu.VMEM((terms, slots, 2 * width), BF16),
            pltpu.VMEM((terms, SLOT, width), F32),
            pltpu.VMEM((24, width), F32),
            pltpu.VMEM((8, width), F32),
            pltpu.VMEM((8, width), F32),
            pltpu.VMEM((chaos_n, 8, width), F32),
            pltpu.VMEM((space_n, 8, width), F32),
            pltpu.SemaphoreType.DMA((4,)),
            pltpu.SemaphoreType.DMA((30,)),
            pltpu.SemaphoreType.DMA((4, chaos_n)),
            pltpu.SemaphoreType.DMA((4, chaos_n)),
            pltpu.SemaphoreType.DMA((2, chaos_n)),
            pltpu.SemaphoreType.DMA((chaos_n,)),
            pltpu.SemaphoreType.DMA((space_n,)),
        ],
        compiler_params=pltpu.CompilerParams(
            collective_id=0, has_side_effects=True, vmem_limit_bytes=60 * 1024 * 1024
        ),
    )(
        start_field.reshape(own_modes, rows, width),
        source_term.reshape(own_modes, rows, width),
        conductivity.reshape(terms + 1, rows, width),
        lists,
    )
    return tuple(out.reshape(source_term.shape) for out in outs)


def solution(mesh):
    chaos_n, space_n = (mesh.shape["chaos"], mesh.shape["space"])
    field = P("chaos", "space", None, None)
    return jax.shard_map(
        functools.partial(per_device, chaos_n, space_n),
        mesh=mesh,
        in_specs=(field, field, P(None, "space", None, None), P(), P()),
        out_specs=(field, field, field),
        check_vma=False,
    )
```

time: 134 us -> 145 us (1.082)
  Pallas kernels: 128 us -> 138 us
    pallas_call x1, Pallas kernels: 128 us -> 138 us  [per_device(): pl.pallas_call(functools.partial(kernel, chaos_n, space_n, terms, own_mod...]
where the time goes in v2:
time: 145 us
  Pallas kernels  138 us (95%)
  local copies, waits for them, and re-layouts  4.6 us (3%)
    pallas_call x1, Pallas kernels, per_device(): pl.pallas_call(functools.partial(kernel, chaos_n, space_n, terms, own_mod...  138 us
    unnamed x9, local copies, waits for them, and re-layouts  4.6 us

profile of v2, /device:TPU:1, one launch (start us, length us, event | category | flops | bytes accessed | tf_op | source)
XLA Modules:
  0.0 144.9 jit_solution(17732685267875645084)
XLA Ops:
  0.6 0.8 fusion
  1.4 0.0 copy-start.2
  1.4 0.7 copy-done.2
  2.1 0.6 select_maximum_fusion.lists_ref
  2.8 138.2 %shard_map.76 = (f32[15,64,128]{2,1,0:T(8,128)}, f32[15,64,128]{2,1,0:T(8,128)}, f32[15,64,128]{2,1,0:T(8,128)}) custom-call(f32[15,64,128]{2,1,0:T(8,128)} %bitcast.19, f32[15,64,128]{2,1,0:T(8,128)} %bitcast.20, f32[9,64,128]{2,1,0:T(8,128)} %bitcast.21, f32[24,512]{1,0:T(8,128)} %select_maximum_fusion.lists_ref), custom_call_target="tpu_custom_call" | custom-call | tf_op jit(solution)/shard_map/pallas_call | solution.py:545
  140.9 0.0 copy-start.1
  141.0 1.9 %copy.19 = f32[15,1,64,128]{3,2,1,0:T(8,128)} copy(f32[15,1,64,128]{3,2,1,0:T(8,128)} %bitcast.18) | data formatting | bytes 983040
  142.9 0.0 copy-done.1
  142.9 0.0 copy-start
  142.9 0.8 copy.20
  143.7 0.4 copy-done
  144.1 0.8 copy.21
  (1 shorter events, 0.0 us)
Async XLA Ops:
  1.4 0.7 copy-start.2
  140.9 1.9 %copy-start.1 = (f32[15,64,128]{2,1,0:T(8,128)S(1)}, f32[15,64,128]{2,1,0:T(8,128)}, u32[]{:S(2)}) copy-start(f32[15,64,128]{2,1,0:T(8,128)} %get-tuple-element.7) | copy-start | bytes 1474564
  142.9 1.2 copy-start

commit v3 on v2

--- a/solution.py
+++ b/solution.py
@@ -44,8 +44,8 @@
     flat = rows * SLOT
     width = v_ref.shape[-1]
     tiles = rows // 8
-    per = -(-chaos_n // (terms // 2))
-    lag = max(2, chaos_n // 4)
+    per = -(-chaos_n // terms)
+    lag = max(2, chaos_n // 2)
 
     def swing(i):
         return (2 * lax.rem(i, 2) - 1) * ((i + 1) // 2)
@@ -176,7 +176,16 @@
 
     scatter(xv, tv, 0)
     turn_in(f_ref, xf)
-    scatter(xf, tf, 1)
+    tf[block(me), :] = xf[block(me), :]
+
+    def send_source(i):
+        @pl.when(i > 0)
+        def _():
+            c = target(i)
+            remote(
+                xf.at[block(c)], tf.at[block(me)], send_sem.at[5], a2a_sem.at[1].at[me], {"chaos": c}
+            ).start()
+
 
     lane = lax.broadcasted_iota(jnp.int32, (1, width), 1)
     zm_mask = jnp.where(lane > 0, 0.5, 0.0).astype(F32)
@@ -304,14 +313,15 @@
         gl[j] = (g - top.astype(F32)).astype(BF16)
 
         def step(n, inner):
-            i = (j - terms // 2) * per + n
-
-            @pl.when(i >= 0)
+            i = j * per + n
+
+            @pl.when(i < chaos_n)
             def _():
                 arrived(tv, 0, i)
                 spread_halo(tv, (vxm, vxp, vym, vyp), 0, i)
-
-            @pl.when(i >= lag)
+                send_source(i)
+
+            @pl.when((i >= lag) & (i < chaos_n))
             def _():
                 products(tv, (vxm, vxp, vym, vyp), 0, y0, i - lag)
 
@@ -366,22 +376,16 @@
                 weigh(0, value * tr[at, :])
         spread_halo(ts, (sxm, sxp, sym, syp), 2, i)
 
-    def chain(i, carry):
-        @pl.when(i < chaos_n)
-        def _():
-            residual_step(i)
-
-        @pl.when((i >= lag) & (i < chaos_n + lag))
-        def _():
-            search_step(i - lag)
-
-        @pl.when(i >= 2 * lag)
-        def _():
-            products(ts, (sxm, sxp, sym, syp), 2, y1, i - 2 * lag)
-
-        return carry
-
-    lax.fori_loop(0, chaos_n + 2 * lag, chain, 0)
+    def each(step):
+        def body(i, carry):
+            step(i)
+            return carry
+
+        lax.fori_loop(0, chaos_n, body, 0)
+
+    each(residual_step)
+    each(search_step)
+    each(lambda i: products(ts, (sxm, sxp, sym, syp), 2, y1, i))
     rr[block(me), :] = tr[block(me), :]
     mix(y1)
     scatter(y1, qq, 3)
@@ -474,6 +478,8 @@
 
     slab_finish(zr, zrm, zrp, 0, ss)
 
+    slab_step(qq, 3, zq, zqm, zqp, 26, 1)
+
     def hear(k, total):
         remote(dots, dga.at[k], send_sem.at[28], dota_sem.at[k], {"chaos": left}).wait_recv()
         return total + dga[k]
@@ -487,7 +493,6 @@
 
     lax.fori_loop(1, space_n, tell_space, 0)
 
-    slab_step(qq, 3, zq, zqm, zqp, 26, 1)
     slab_finish(zq, zqm, zqp, 1, mq)
 
     def hear_space(k, total):

time: 145 us -> 122 us (0.84)
  Pallas kernels: 138 us -> 115 us
    pallas_call x1, Pallas kernels: 138 us -> 115 us  [per_device(): pl.pallas_call(functools.partial(kernel, chaos_n, space_n, terms, own_mod...]
where the time goes in v3:
time: 122 us
  Pallas kernels  115 us (94%)
  local copies, waits for them, and re-layouts  4.6 us (4%)
  other arithmetic  1.42 us (1%)
    pallas_call x1, Pallas kernels, per_device(): pl.pallas_call(functools.partial(kernel, chaos_n, space_n, terms, own_mod...  115 us
    unnamed x9, local copies, waits for them, and re-layouts  4.6 us

profile of v3, /device:TPU:1, one launch (start us, length us, event | category | flops | bytes accessed | tf_op | source)
XLA Modules:
  0.0 121.9 jit_solution(13452811271195932323)
XLA Ops:
  0.6 0.8 fusion
  1.4 0.0 copy-start.2
  1.4 0.7 copy-done.2
  2.1 0.6 select_maximum_fusion.lists_ref
  2.8 115.2 %shard_map.76 = (f32[15,64,128]{2,1,0:T(8,128)}, f32[15,64,128]{2,1,0:T(8,128)}, f32[15,64,128]{2,1,0:T(8,128)}) custom-call(f32[15,64,128]{2,1,0:T(8,128)} %bitcast.19, f32[15,64,128]{2,1,0:T(8,128)} %bitcast.20, f32[9,64,128]{2,1,0:T(8,128)} %bitcast.21, f32[24,512]{1,0:T(8,128)} %select_maximum_fusion.lists_ref), custom_call_target="tpu_custom_call" | custom-call | tf_op jit(solution)/shard_map/pallas_call | solution.py:550
  118.0 0.0 copy-start.1
  118.0 1.9 %copy.19 = f32[15,1,64,128]{3,2,1,0:T(8,128)} copy(f32[15,1,64,128]{3,2,1,0:T(8,128)} %bitcast.18) | data formatting | bytes 983040
  119.9 0.0 copy-done.1
  119.9 0.0 copy-start
  119.9 0.8 copy.20
  120.7 0.4 copy-done
  121.1 0.8 copy.21
  (1 shorter events, 0.0 us)
Async XLA Ops:
  1.4 0.7 copy-start.2
  118.0 1.9 %copy-start.1 = (f32[15,64,128]{2,1,0:T(8,128)S(1)}, f32[15,64,128]{2,1,0:T(8,128)}, u32[]{:S(2)}) copy-start(f32[15,64,128]{2,1,0:T(8,128)} %get-tuple-element.7) | copy-start | bytes 1474564
  119.9 1.2 copy-start

commit v4 on v3

--- a/solution.py
+++ b/solution.py
@@ -24,8 +24,8 @@
 def kernel(
     chaos_n, space_n, terms, own_modes, rows,
     v_ref, f_ref, cond_ref, lists_ref,
-    sol_ref, res_ref, dir_ref,
-    xv, xf, rr, ss, qq, mq, zr, zrm, zrp, zq, zqm, zqp,
+    ss, mq, rr_ref, qq_ref, scale_ref,
+    xv, xf, rr, qq, zr, zrm, zrp, zq, zqm, zqp,
     tv, tf, tr, tz, ts, tw, y0, y1,
     vxm, vxp, zxm, zxp, sxm, sxp, wxm, wxp,
     vym, vyp, zym, zyp, sym, syp, wym, wyp,
@@ -296,6 +296,8 @@
     def build(j, carry):
         first = lists_ref[pl.ds(j, 1), :]
         second = lists_ref[pl.ds(j + terms, 1), :]
+        first = first + (SLOT - own_modes) * jnp.floor((first + 0.5) * (1.0 / own_modes))
+        second = second + (SLOT - own_modes) * jnp.floor((second + 0.5) * (1.0 / own_modes))
         weight = lists_ref[pl.ds(j + 2 * terms, 1), :]
         weight_high = weight.astype(BF16).astype(F32)
         weight_low = weight - weight_high
@@ -355,12 +357,6 @@
                 tz[at, :] = value * inv
         spread_halo(tz, (zxm, zxp, zym, zyp), 1, i)
 
-        @pl.when(i > 0)
-        def _():
-            remote(
-                tr.at[block(c)], rr.at[block(me)], send_sem.at[6], a2a_sem.at[2].at[me], {"chaos": c}
-            ).start()
-
     def search_step(i):
         halo_arrived(1, i)
         c = source(i)
@@ -385,7 +381,19 @@
 
     each(residual_step)
     each(search_step)
-    each(lambda i: products(ts, (sxm, sxp, sym, syp), 2, y1, i))
+
+    def last_step(i):
+        c = source(i)
+
+        @pl.when(i > 0)
+        def _():
+            remote(
+                tr.at[block(c)], rr.at[block(me)], send_sem.at[6], a2a_sem.at[2].at[me], {"chaos": c}
+            ).start()
+
+        products(ts, (sxm, sxp, sym, syp), 2, y1, i)
+
+    each(last_step)
     rr[block(me), :] = tr[block(me), :]
     mix(y1)
     scatter(y1, qq, 3)
@@ -418,7 +426,7 @@
 
         lax.fori_loop(0, chaos_n, body, 0)
 
-    def slab_finish(z, zm, zp, number, to):
+    def slab_finish(z, zm, zp, number, to, field, keep):
         def body(i, carry):
             c = source(i)
             pltpu.make_async_copy(xv.at[pl.ds(0, 64)], xv.at[pl.ds(0, 64)], slab_sem.at[number].at[c]).wait()
@@ -442,6 +450,7 @@
                     for n in range(6):
                         value = value + coef[n] * near[n]
                     to[at, :] = value
+                    keep[at, :] = field[at, :]
             return carry
 
         lax.fori_loop(0, chaos_n, body, 0)
@@ -476,7 +485,7 @@
 
     lax.fori_loop(1, chaos_n, tell, 0)
 
-    slab_finish(zr, zrm, zrp, 0, ss)
+    slab_finish(zr, zrm, zrp, 0, ss, rr, rr_ref)
 
     slab_step(qq, 3, zq, zqm, zqp, 26, 1)
 
@@ -493,7 +502,7 @@
 
     lax.fori_loop(1, space_n, tell_space, 0)
 
-    slab_finish(zq, zqm, zqp, 1, mq)
+    slab_finish(zq, zqm, zqp, 1, mq, qq, qq_ref)
 
     def hear_space(k, total):
         remote(dsum, dgb.at[k], send_sem.at[29], dotb_sem.at[k], {"space": up}).wait_recv()
@@ -505,20 +514,8 @@
     step_size = energy_start / curvature
     energy_next = energy_start - 2.0 * step_size * curvature + step_size * step_size * image_energy
     ratio = 1.0 + energy_next / energy_start
-    step_all = jnp.broadcast_to(step_size, (8, width))
-    ratio_all = jnp.broadcast_to(ratio, (8, width))
-
-    def turn_out(m, carry):
-        for tile in range(tiles):
-            where = pl.ds(tile * 128 + m, 8, stride=SLOT)
-            there = pl.ds(tile * 8, 8)
-            search = ss[where, :]
-            sol_ref[m, there, :] = v_ref[m, there, :] + step_all * search
-            res_ref[m, there, :] = rr[where, :] - step_all * qq[where, :]
-            dir_ref[m, there, :] = ratio_all * search - step_all * mq[where, :]
-        return carry
-
-    lax.fori_loop(0, own_modes, turn_out, 0)
+    scale_ref[pl.ds(0, 8), :] = jnp.broadcast_to(step_size, (8, width))
+    scale_ref[pl.ds(8, 8), :] = jnp.broadcast_to(ratio, (8, width))
 
     for n, ref in enumerate((xv, xf, tr, y1)):
         drain(ref, (chaos_n - 1) * 32, send_sem.at[4 + n])
@@ -532,27 +529,46 @@
     pltpu.make_async_copy(dgb.at[pl.ds(1, space_n - 1)], dgb.at[pl.ds(1, space_n - 1)], send_sem.at[29]).wait()
 
 
+def combine(own_modes, v_ref, ss, rr, qq, mq, scale_ref, sol_ref, res_ref, dir_ref):
+    step_all = scale_ref[pl.ds(0, 8), :]
+    ratio_all = scale_ref[pl.ds(8, 8), :]
+    tiles = v_ref.shape[1] // 8
+
+    def turn_out(m, carry):
+        for tile in range(tiles):
+            where = pl.ds(tile * 128 + m, 8, stride=SLOT)
+            there = pl.ds(tile * 8, 8)
+            search = ss[where, :]
+            sol_ref[m, there, :] = v_ref[m, there, :] + step_all * search
+            res_ref[m, there, :] = rr[where, :] - step_all * qq[where, :]
+            dir_ref[m, there, :] = ratio_all * search - step_all * mq[where, :]
+        return carry
+
+    lax.fori_loop(0, own_modes, turn_out, 0)
+
+
 def per_device(chaos_n, space_n, source_term, start_field, conductivity, pair_modes, pair_weight):
     own_modes, _, rows, width = source_term.shape
     terms, pairs = pair_weight.shape
     slots = chaos_n * SLOT
     flat = rows * SLOT
     padded = -(-pairs // 128) * 128
-    ends = pair_modes + pair_modes // own_modes * (SLOT - own_modes)
     lists = jnp.concatenate(
-        [ends[:, :, 0].astype(F32), ends[:, :, 1].astype(F32), pair_weight], axis=0
+        [pair_modes[:, :, 0].astype(F32), pair_modes[:, :, 1].astype(F32), pair_weight], axis=0
     )
     lists = jnp.pad(lists, ((0, 0), (0, padded - pairs)), constant_values=-1.0)
     field = pltpu.VMEM((flat, width), F32)
     half = pltpu.VMEM((flat // 2, width), F32)
     vmem = pl.BlockSpec(memory_space=pltpu.VMEM)
     shape = jax.ShapeDtypeStruct((own_modes, rows, width), F32)
-    outs = pl.pallas_call(
+    flat_shape = jax.ShapeDtypeStruct((flat, width), F32)
+    start = start_field.reshape(own_modes, rows, width)
+    search, precond, residual, image, scale = pl.pallas_call(
         functools.partial(kernel, chaos_n, space_n, terms, own_modes, rows),
-        out_shape=(shape, shape, shape),
+        out_shape=(flat_shape,) * 4 + (jax.ShapeDtypeStruct((16, width), F32),),
         in_specs=[vmem] * 4,
-        out_specs=(vmem, vmem, vmem),
-        scratch_shapes=[field] * 28
+        out_specs=(vmem,) * 5,
+        scratch_shapes=[field] * 26
         + [half] * 8
         + [field]
         + [pltpu.VMEM((32, width), F32)] * 2
@@ -588,11 +604,21 @@
             collective_id=0, has_side_effects=True, vmem_limit_bytes=60 * 1024 * 1024
         ),
     )(
-        start_field.reshape(own_modes, rows, width),
+        start,
         source_term.reshape(own_modes, rows, width),
         conductivity.reshape(terms + 1, rows, width),
         lists,
     )
+    split = 4 if rows % 32 == 0 else 1
+    plain = pl.BlockSpec((own_modes, rows // split, width), lambda n: (0, n, 0))
+    turned = pl.BlockSpec((flat // split, width), lambda n: (n, 0))
+    outs = pl.pallas_call(
+        functools.partial(combine, own_modes),
+        grid=(split,),
+        out_shape=(shape,) * 3,
+        in_specs=[plain] + [turned] * 4 + [pl.BlockSpec((16, width), lambda n: (0, 0))],
+        out_specs=(plain,) * 3,
+    )(start, search, residual, image, precond, scale)
     return tuple(out.reshape(source_term.shape) for out in outs)
 
 

time: 122 us -> 114 us (0.934)
  Pallas kernels: 115 us -> 111 us
  local copies, waits for them, and re-layouts: 4.6 us -> 1.56 us
    pallas_call x1, Pallas kernels: 115 us -> 106 us  [per_device(): pl.pallas_call(functools.partial(kernel, chaos_n, space_n, terms, own_mod...]
    pallas_call x0 -> x1, Pallas kernels: none -> 4.46 us  [per_device(): pl.pallas_call(functools.partial(combine, own_modes), grid=(split,), out_...]
    unnamed x9 -> x2, local copies, waits for them, and re-layouts: 4.6 us -> 0.7 us
where the time goes in v4:
time: 114 us
  Pallas kernels  111 us (97%)
  local copies, waits for them, and re-layouts  1.56 us (1%)
    pallas_call x1, Pallas kernels, per_device(): pl.pallas_call(functools.partial(kernel, chaos_n, space_n, terms, own_mod...  106 us
    pallas_call x1, Pallas kernels, per_device(): pl.pallas_call(functools.partial(combine, own_modes), grid=(split,), out_...  4.46 us

profile of v4, /device:TPU:1, one launch (start us, length us, event | category | flops | bytes accessed | tf_op | source)
XLA Modules:
  0.0 113.6 jit_solution(11926539311232012623)
XLA Ops:
  0.6 0.9 fusion.2
  1.5 0.0 copy-start
  1.5 0.7 copy-done
  2.2 0.6 select_maximum_fusion.lists_ref
  2.8 106.3 %shard_map.76 = (f32[1024,128]{1,0:T(8,128)}, f32[1024,128]{1,0:T(8,128)}, f32[1024,128]{1,0:T(8,128)}, f32[1024,128]{1,0:T(8,128)}, f32[16,128]{1,0:T(8,128)}) custom-call(f32[15,64,128]{2,1,0:T(8,128)} %bitcast.16, f32[15,64,128]{2,1,0:T(8,128)} %bitcast.18, f32[9,64,128]{2,1,0:T(8,128)} %bitcast.19, f32[24,512]{1,0:T(8,128)} %select_maximum_fusion.lists_ref), custom_call_target="tpu_custom_call" | custom-call | tf_op jit(solution)/shard_map/pallas_call | solution.py:566
  109.2 4.5 %shard_map.77 = (f32[15,64,128]{2,1,0:T(8,128)}, f32[15,64,128]{2,1,0:T(8,128)}, f32[15,64,128]{2,1,0:T(8,128)}) custom-call(f32[15,64,128]{2,1,0:T(8,128)} %bitcast.17, f32[1024,128]{1,0:T(8,128)} %get-tuple-element.11.ss, f32[1024,128]{1,0:T(8,128)} %get-tuple-element.12.rr, f32[1024,128]{1,0:T(8,128)} %get-tuple-element.13.qq, ...), custom_call_target="tpu_custom_call" | custom-call | tf_op jit(solution)/shard_map/pallas_call | solution.py:615
  (1 shorter events, 0.0 us)
Async XLA Ops:
  1.5 0.7 copy-start

commit v5 on v4

--- a/solution.py
+++ b/solution.py
@@ -395,8 +395,41 @@
 
     each(last_step)
     rr[block(me), :] = tr[block(me), :]
-    mix(y1)
-    scatter(y1, qq, 3)
+    heights = slots // (4 * SLOT)
+
+    def pick(ref, j, part):
+        return jnp.concatenate(
+            [ref[j, pl.ds((z * 4 + part * 2) * SLOT, 2 * SLOT), :] for z in range(heights)], axis=0
+        )
+
+    for part in range(2):
+
+        def body(j, total):
+            a, b = (pick(gh, j, part), ph[j])
+            total = total + jnp.dot(a, b, preferred_element_type=F32)
+            total = total + jnp.dot(a, plo[j], preferred_element_type=F32)
+            return total + jnp.dot(pick(gl, j, part), b, preferred_element_type=F32)
+
+        total = lax.fori_loop(0, terms, body, jnp.zeros((slots // 2, 2 * width), F32))
+        for n in range(2 * heights):
+            c = n // 2 * 4 + part * 2 + n % 2
+            for r in range(2):
+                at = pl.ds(c * 32 + r * SLOT, SLOT)
+                y1[at, :] = y1[at, :] + total[n * SLOT : (n + 1) * SLOT, r * width : (r + 1) * width]
+
+        def send_image(n, carry):
+            c = target(chaos_n - n)
+
+            @pl.when(lax.rem(c, 4) // 2 == part)
+            def _():
+                remote(
+                    y1.at[block(c)], qq.at[block(me)], send_sem.at[7], a2a_sem.at[3].at[me], {"chaos": c}
+                ).start()
+
+            return carry
+
+        lax.fori_loop(1, chaos_n, send_image, 0)
+    qq[block(me), :] = y1[block(me), :]
 
     def image_step(i, carry):
         c = source(i)
@@ -410,52 +443,44 @@
 
     lax.fori_loop(0, chaos_n, image_step, 0)
 
-    def slab_step(src, which, z, zm, zp, base, number):
-        def body(i, carry):
-            arrived(src, which, i)
-            c = source(i)
-            for r in range(2):
-                inv = ob[pl.ds(al((c * 2 + r) * 56 + 48, 8), 8), :]
-                for h in range(2):
-                    at = pl.ds(al(c * 32 + r * SLOT + h * 8, 8), 8)
-                    z[at, :] = src[at, :] * inv
-            rsem = slab_sem.at[number].at[c]
-            remote(z.at[block(c)], zm.at[block(c)], send_sem.at[base], rsem, {"space": up}).start()
-            remote(z.at[block(c)], zp.at[block(c)], send_sem.at[base + 1], rsem, {"space": down}).start()
-            return carry
-
-        lax.fori_loop(0, chaos_n, body, 0)
-
-    def slab_finish(z, zm, zp, number, to, field, keep):
-        def body(i, carry):
-            c = source(i)
-            pltpu.make_async_copy(xv.at[pl.ds(0, 64)], xv.at[pl.ds(0, 64)], slab_sem.at[number].at[c]).wait()
-            for r in range(2):
-                line = c * 2 + r
-                prev = lax.rem(line + rows - 1, rows)
-                after = lax.rem(line + 1, rows)
-                coef = [ob[pl.ds(al(line * 56 + n * 8, 8), 8), :] for n in range(6)]
-                for h in range(2):
-                    at = pl.ds(al(line * SLOT + h * 8, 8), 8)
-                    v = z[at, :]
-                    near = (
-                        zm[at, :],
-                        zp[at, :],
-                        z[pl.ds(al(prev * SLOT + h * 8, 8), 8), :],
-                        z[pl.ds(al(after * SLOT + h * 8, 8), 8), :],
-                        pltpu.roll(v, 1, 1),
-                        pltpu.roll(v, width - 1, 1),
-                    )
-                    value = (FIRST_COEF - SECOND_COEF) * v
-                    for n in range(6):
-                        value = value + coef[n] * near[n]
-                    to[at, :] = value
-                    keep[at, :] = field[at, :]
-            return carry
-
-        lax.fori_loop(0, chaos_n, body, 0)
-
-    slab_step(rr, 2, zr, zrm, zrp, 24, 0)
+    def slab_step(src, which, z, zm, zp, base, number, i):
+        arrived(src, which, i)
+        c = source(i)
+        for r in range(2):
+            inv = ob[pl.ds(al((c * 2 + r) * 56 + 48, 8), 8), :]
+            for h in range(2):
+                at = pl.ds(al(c * 32 + r * SLOT + h * 8, 8), 8)
+                z[at, :] = src[at, :] * inv
+        rsem = slab_sem.at[number].at[c]
+        remote(z.at[block(c)], zm.at[block(c)], send_sem.at[base], rsem, {"space": up}).start()
+        remote(z.at[block(c)], zp.at[block(c)], send_sem.at[base + 1], rsem, {"space": down}).start()
+
+    def slab_finish(z, zm, zp, number, to, field, keep, i):
+        c = source(i)
+        pltpu.make_async_copy(xv.at[pl.ds(0, 64)], xv.at[pl.ds(0, 64)], slab_sem.at[number].at[c]).wait()
+        for r in range(2):
+            line = c * 2 + r
+            prev = lax.rem(line + rows - 1, rows)
+            after = lax.rem(line + 1, rows)
+            coef = [ob[pl.ds(al(line * 56 + n * 8, 8), 8), :] for n in range(6)]
+            for h in range(2):
+                at = pl.ds(al(line * SLOT + h * 8, 8), 8)
+                v = z[at, :]
+                near = (
+                    zm[at, :],
+                    zp[at, :],
+                    z[pl.ds(al(prev * SLOT + h * 8, 8), 8), :],
+                    z[pl.ds(al(after * SLOT + h * 8, 8), 8), :],
+                    pltpu.roll(v, 1, 1),
+                    pltpu.roll(v, width - 1, 1),
+                )
+                value = (FIRST_COEF - SECOND_COEF) * v
+                for n in range(6):
+                    value = value + coef[n] * near[n]
+                to[at, :] = value
+                keep[at, :] = field[at, :]
+
+    each(lambda i: slab_step(rr, 2, zr, zrm, zrp, 24, 0, i))
 
     def image_dot(i, carry):
         halo_arrived(3, i)
@@ -485,9 +510,23 @@
 
     lax.fori_loop(1, chaos_n, tell, 0)
 
-    slab_finish(zr, zrm, zrp, 0, ss, rr, rr_ref)
-
-    slab_step(qq, 3, zq, zqm, zqp, 26, 1)
+    each(lambda i: slab_finish(zr, zrm, zrp, 0, ss, rr, rr_ref, i))
+
+    slack = max(2, chaos_n // 4)
+    turn = chaos_n - slack
+
+    def tail(n, carry):
+        @pl.when(n < chaos_n)
+        def _():
+            slab_step(qq, 3, zq, zqm, zqp, 26, 1, chaos_n - 1 - n)
+
+        @pl.when(n >= slack)
+        def _():
+            slab_finish(zq, zqm, zqp, 1, mq, qq, qq_ref, chaos_n - 1 - n + slack)
+
+        return carry
+
+    lax.fori_loop(0, turn, tail, 0)
 
     def hear(k, total):
         remote(dots, dga.at[k], send_sem.at[28], dota_sem.at[k], {"chaos": left}).wait_recv()
@@ -502,7 +541,7 @@
 
     lax.fori_loop(1, space_n, tell_space, 0)
 
-    slab_finish(zq, zqm, zqp, 1, mq, qq, qq_ref)
+    lax.fori_loop(turn, chaos_n + slack, tail, 0)
 
     def hear_space(k, total):
         remote(dsum, dgb.at[k], send_sem.at[29], dotb_sem.at[k], {"space": up}).wait_recv()

time: 114 us -> 116 us (1.018)
  Pallas kernels: 111 us -> 113 us
    pallas_call x1, Pallas kernels: 106 us -> 108 us  [per_device(): pl.pallas_call(functools.partial(kernel, chaos_n, space_n, terms, own_mod...]
where the time goes in v5:
time: 116 us
  Pallas kernels  113 us (97%)
  local copies, waits for them, and re-layouts  1.56 us (1%)
    pallas_call x1, Pallas kernels, per_device(): pl.pallas_call(functools.partial(kernel, chaos_n, space_n, terms, own_mod...  108 us
    pallas_call x1, Pallas kernels, per_device(): pl.pallas_call(functools.partial(combine, own_modes), grid=(split,), out_...  4.46 us

profile of v5, /device:TPU:1, one launch (start us, length us, event | category | flops | bytes accessed | tf_op | source)
XLA Modules:
  0.0 115.8 jit_solution(5503571590256127909)
XLA Ops:
  0.6 0.9 fusion.2
  1.5 0.0 copy-start
  1.5 0.7 copy-done
  2.2 0.6 select_maximum_fusion.lists_ref
  2.8 108.5 %shard_map.76 = (f32[1024,128]{1,0:T(8,128)}, f32[1024,128]{1,0:T(8,128)}, f32[1024,128]{1,0:T(8,128)}, f32[1024,128]{1,0:T(8,128)}, f32[16,128]{1,0:T(8,128)}) custom-call(f32[15,64,128]{2,1,0:T(8,128)} %bitcast.16, f32[15,64,128]{2,1,0:T(8,128)} %bitcast.18, f32[9,64,128]{2,1,0:T(8,128)} %bitcast.19, f32[24,512]{1,0:T(8,128)} %select_maximum_fusion.lists_ref), custom_call_target="tpu_custom_call" | custom-call | tf_op jit(solution)/shard_map/pallas_call | solution.py:605
  111.3 4.5 %shard_map.77 = (f32[15,64,128]{2,1,0:T(8,128)}, f32[15,64,128]{2,1,0:T(8,128)}, f32[15,64,128]{2,1,0:T(8,128)}) custom-call(f32[15,64,128]{2,1,0:T(8,128)} %bitcast.17, f32[1024,128]{1,0:T(8,128)} %get-tuple-element.11.ss, f32[1024,128]{1,0:T(8,128)} %get-tuple-element.12.rr, f32[1024,128]{1,0:T(8,128)} %get-tuple-element.13.qq, ...), custom_call_target="tpu_custom_call" | custom-call | tf_op jit(solution)/shard_map/pallas_call | solution.py:654
  (1 shorter events, 0.0 us)
Async XLA Ops:
  1.5 0.7 copy-start

commit v6 on v4

--- a/solution.py
+++ b/solution.py
@@ -23,7 +23,7 @@
 
 def kernel(
     chaos_n, space_n, terms, own_modes, rows,
-    v_ref, f_ref, cond_ref, lists_ref,
+    v_ref, f_ref, cond_ref, modes_ref, weight_ref,
     ss, mq, rr_ref, qq_ref, scale_ref,
     xv, xf, rr, qq, zr, zrm, zrp, zq, zqm, zqp,
     tv, tf, tr, tz, ts, tw, y0, y1,
@@ -31,7 +31,7 @@
     vym, vyp, zym, zyp, sym, syp, wym, wyp,
     cy, cxm, cxp, c0m, c0p, oc, ob, kf, kb, tb,
     gh, gl, oa, wh, wl, ph, plo, acc,
-    sums, dots, dsum, dga, dgb,
+    lists_ref, sums, dots, dsum, dga, dgb,
     coef_sem, send_sem, a2a_sem, halo_sem, slab_sem, dota_sem, dotb_sem,
 ):
     me = lax.axis_index("chaos")
@@ -45,7 +45,7 @@
     width = v_ref.shape[-1]
     tiles = rows // 8
     per = -(-chaos_n // terms)
-    lag = max(2, chaos_n // 2)
+    lag = chaos_n
 
     def swing(i):
         return (2 * lax.rem(i, 2) - 1) * ((i + 1) // 2)
@@ -290,6 +290,12 @@
                 at = pl.ds(c * 32 + r * SLOT, SLOT)
                 y[at, :] = y[at, :] + total[c * SLOT : (c + 1) * SLOT, r * width : (r + 1) * width]
 
+    pairs = weight_ref.shape[-1]
+    lists_ref[...] = jnp.full_like(lists_ref, -1.0)
+    for n in range(2):
+        lists_ref[pl.ds(n * terms, terms), pl.ds(0, pairs)] = modes_ref[n].astype(F32)
+    lists_ref[pl.ds(2 * terms, terms), pl.ds(0, pairs)] = weight_ref[...]
+
     index = lax.broadcasted_iota(jnp.int32, (slots, lists_ref.shape[-1]), 0).astype(F32)
     nt = (((1,), (1,)), ((), ()))
 
@@ -553,10 +559,6 @@
     slots = chaos_n * SLOT
     flat = rows * SLOT
     padded = -(-pairs // 128) * 128
-    lists = jnp.concatenate(
-        [pair_modes[:, :, 0].astype(F32), pair_modes[:, :, 1].astype(F32), pair_weight], axis=0
-    )
-    lists = jnp.pad(lists, ((0, 0), (0, padded - pairs)), constant_values=-1.0)
     field = pltpu.VMEM((flat, width), F32)
     half = pltpu.VMEM((flat // 2, width), F32)
     vmem = pl.BlockSpec(memory_space=pltpu.VMEM)
@@ -566,7 +568,7 @@
     search, precond, residual, image, scale = pl.pallas_call(
         functools.partial(kernel, chaos_n, space_n, terms, own_modes, rows),
         out_shape=(flat_shape,) * 4 + (jax.ShapeDtypeStruct((16, width), F32),),
-        in_specs=[vmem] * 4,
+        in_specs=[vmem] * 5,
         out_specs=(vmem,) * 5,
         scratch_shapes=[field] * 26
         + [half] * 8
@@ -587,6 +589,7 @@
             pltpu.VMEM((terms, slots, 2 * width), BF16),
             pltpu.VMEM((terms, slots, 2 * width), BF16),
             pltpu.VMEM((terms, SLOT, width), F32),
+            pltpu.VMEM((3 * terms, padded), F32),
             pltpu.VMEM((24, width), F32),
             pltpu.VMEM((8, width), F32),
             pltpu.VMEM((8, width), F32),
@@ -607,9 +610,10 @@
         start,
         source_term.reshape(own_modes, rows, width),
         conductivity.reshape(terms + 1, rows, width),
-        lists,
+        jnp.transpose(pair_modes, (2, 0, 1)),
+        pair_weight,
     )
-    split = 4 if rows % 32 == 0 else 1
+    split = 2 if rows % 16 == 0 else 1
     plain = pl.BlockSpec((own_modes, rows // split, width), lambda n: (0, n, 0))
     turned = pl.BlockSpec((flat // split, width), lambda n: (n, 0))
     outs = pl.pallas_call(

time: 114 us -> 112 us (0.982)
  no operation moved by 1% of the time
where the time goes in v6:
time: 112 us
  Pallas kernels  110 us (98%)
  local copies, waits for them, and re-layouts  1.38 us (1%)
    pallas_call x1, Pallas kernels, per_device(): pl.pallas_call(functools.partial(kernel, chaos_n, space_n, terms, own_mod...  106 us
    pallas_call x1, Pallas kernels, per_device(): pl.pallas_call(functools.partial(combine, own_modes), grid=(split,), out_...  3.46 us

profile of v6, /device:TPU:1, one launch (start us, length us, event | category | flops | bytes accessed | tf_op | source)
XLA Modules:
  0.0 111.8 jit_solution(16449008680817729539)
XLA Ops:
  0.6 1.4 %copy.13 = s32[8,480,2]{1,0,2:T(8,128)} copy(s32[8,480,2]{1,2,0:T(2,128)} %param.8) | data formatting | bytes 61440 | tf_op args[3]
  2.0 106.3 %shard_map.76 = (f32[1024,128]{1,0:T(8,128)}, f32[1024,128]{1,0:T(8,128)}, f32[1024,128]{1,0:T(8,128)}, f32[1024,128]{1,0:T(8,128)}, f32[16,128]{1,0:T(8,128)}) custom-call(f32[15,64,128]{2,1,0:T(8,128)} %bitcast.15, f32[15,64,128]{2,1,0:T(8,128)} %bitcast.17, f32[9,64,128]{2,1,0:T(8,128)} %bitcast.18, s32[2,8,480]{2,1,0:T(8,128)} %bitcast.19, ...), custom_call_target="tpu_custom_call" | custom-call | tf_op jit(solution)/shard_map/pallas_call | solution.py:568
  108.3 3.5 %shard_map.77 = (f32[15,64,128]{2,1,0:T(8,128)}, f32[15,64,128]{2,1,0:T(8,128)}, f32[15,64,128]{2,1,0:T(8,128)}) custom-call(f32[15,64,128]{2,1,0:T(8,128)} %bitcast.16, f32[1024,128]{1,0:T(8,128)} %get-tuple-element.11.ss, f32[1024,128]{1,0:T(8,128)} %get-tuple-element.12.rr, f32[1024,128]{1,0:T(8,128)} %get-tuple-element.13.qq, ...), custom_call_target="tpu_custom_call" | custom-call | tf_op jit(solution)/shard_map/pallas_call | solution.py:619
